TPU v7x, 32 devices: a whole 2x2x4 slice. The times are simulated.
32 devices in a mesh: groups: 2 (over y), tm: 8 (over z, x), space: 2 (over core).
Axes of the slice: x: 2, y: 2, z: 4, core: 2. Of those that a mesh axis runs over, the one named last changes fastest.
Arguments:
- interior_diag: bfloat16 [24576, 1536], P(('groups', 'tm'), 'space'), parts along dimension 0, may hold values from -1 to 5, as said below
- coupling: bfloat16 [24576, 1536], P(('groups', 'tm'), 'space'), parts along dimension 0, may hold values from -0.29882812 to 0.29882812
- arrow_rows: bfloat16 [12288, 1536], P(('groups', 'tm', 'space')), parts along dimension 0, may hold values from -0.59765625 to 0.59765625
- separator_diag: bfloat16 [24576, 1536], P(('groups', 'tm'), 'space'), parts along dimension 0, may hold values from -1 to 5, as said below
- tip: bfloat16 [1536, 768], P('groups', 'space'), parts along dimension 0, may hold values from -6 to 6
- lengths: int32 [16], P('groups'), parts along dimension 0, may hold values from 1 to 2, 12 in all
Outputs:
- new_separator: bfloat16 [24576, 1536], P(('groups', 'tm'), 'space'), parts along dimension 0
- arrow_fill: bfloat16 [12288, 1536], P(('groups', 'tm'), 'space'), parts along dimension 0
- new_tip: float32 [1536, 768], P('groups', 'space'), parts along dimension 0
There are 2 independent parts, one for each index of `groups`. A program takes and returns all parts, laid end to end along the dimension named above; each array names one. Nothing has to cross between parts.
Inputs may be any that keep to these rules, and one draw needn't show every extreme that they name: `interior_diag`: each block of 1536 rows is symmetric with eigenvalues above 0.5. `separator_diag`: each block of 1536 rows is symmetric with eigenvalues above 0.5. `lengths`: partition p has an interior block exactly when entry p is 2; some entry is 2.
All inputs are finite; a program needn't handle non-finite values.
Results may differ from a plain program's by a relative error of at most 0.008.
Values may be sent and summed in bfloat16 or wider, within the bound.
No kernel may reach another device: no remote copies, remote signals or barrier semaphores. Data moves between devices by JAX's collectives and lax.ppermute only.
A program may use at most 128 MiB of HBM per device.

v0:
```python
import functools

import jax
import jax.numpy as jnp
from jax import lax
from jax.experimental import pallas as pl
from jax.experimental.pallas import tpu as pltpu
from jax.sharding import PartitionSpec as P


F32 = jnp.float32
BF16 = jnp.bfloat16
BLOCK = 256
NEAR = 0.03
MOST_STEPS = 60
STAGES = 7
PAD = 16
PIECES = 3


def split(x):
    high = x.astype(BF16)
    return high, (x - high.astype(F32)).astype(BF16)


def nn(a, b):
    return lax.dot_general(a, b, (((1,), (0,)), ((), ())), preferred_element_type=F32)


def nt(a, b):
    return lax.dot_general(a, b, (((1,), (1,)), ((), ())), preferred_element_type=F32)


def three(dot, a, b):
    return dot(a[0], b[0]) + (dot(a[0], b[1]) + dot(a[1], b[0]))


def total(x):
    return jnp.sum(x, keepdims=True)


def places(size):
    rows = lax.broadcasted_iota(jnp.int32, (size, size), 0)
    columns = lax.broadcasted_iota(jnp.int32, (size, size), 1)
    return rows, columns


def diagonal_row(x, on_diagonal):
    return jnp.sum(jnp.where(on_diagonal, x, 0.0), axis=0, keepdims=True)


def unit_scaled(a, on_diagonal):
    diagonal = jnp.where(on_diagonal, a, 0.0)
    scale_row = lax.rsqrt(jnp.sum(diagonal, axis=0, keepdims=True))
    scale_column = lax.rsqrt(jnp.sum(diagonal, axis=1, keepdims=True))
    return a * scale_row * scale_column, scale_row


def first_root(off, off_square, identity):
    bound = jnp.sqrt(jnp.sqrt(total(off_square * off_square)))
    c = jnp.minimum(1.0, 1.9 / (1.0 + bound))
    gap = c * off - (1.0 - c) * identity
    gap_square = c * c * off_square - (2 * c * (1 - c)) * off + ((1 - c) * (1 - c)) * identity
    return (jnp.sqrt(c) * (identity - 0.5 * gap + 0.375 * gap_square)).astype(BF16)


def root_stages(a, on_diagonal, identity, result):
    unit, scale_row = unit_scaled(a, on_diagonal)
    off = unit - identity
    off_high = off.astype(BF16)
    high, low = split(unit)
    yield
    off_square = nn(off_high, off_high)
    yield
    first = first_root(off, off_square, identity)
    yield
    product = split(nt(high, first) + nt(low, first))
    yield
    gap = nn(first, product[0]) + nn(first, product[1]) - identity
    gap_high = gap.astype(BF16)
    yield
    gap_square = nn(gap_high, gap_high)
    change = split(0.375 * gap_square - 0.5 * gap)
    yield
    root = first.astype(F32) + (nn(change[0], first) + nn(change[1], first))
    result.append(split(root * scale_row))
    result.append(gap_square)


def root_until_near(a, on_diagonal, identity, unit_ref, root_ref):
    unit, scale_row = unit_scaled(a, on_diagonal)
    off = unit - identity
    off_square = nn(off.astype(BF16), off.astype(BF16))
    unit_ref[...] = unit
    root_ref[...] = first_root(off, off_square, identity).astype(F32)

    def far(state):
        return jnp.logical_and(jnp.logical_not(state[0] <= NEAR**4), state[1] < MOST_STEPS)

    def step(state):
        root = split(root_ref[...])
        product = split(three(nt, split(unit_ref[...]), root))
        gap = three(nn, root, product) - identity
        gap_square = nn(gap.astype(BF16), gap.astype(BF16))
        change = split(0.375 * gap_square - 0.5 * gap)
        root_ref[...] += three(nn, change, root)
        return jnp.sum(gap_square * gap_square), state[1] + 1

    lax.while_loop(far, step, (jnp.float32(1.0), jnp.int32(0)))
    return split(root_ref[...] * scale_row)


def interleave(stages, fillers):
    share = -(-len(fillers) // STAGES)
    for _ in stages:
        for filler in fillers[:share]:
            filler()
        fillers = fillers[share:]
    for filler in fillers:
        filler()


def eliminate_kernel(
    flags, own_d, other_d, e_hbm, r_hbm, solved_e, solved_r, corner_out, folded_out,
    given, diag, e_in, r_in, left_e, left_r, high, low, high_t, low_t, turned,
    near, unit_ref, root_ref, sems,
):
    size, block = diag.shape[0], unit_ref.shape[0]
    half, width = own_d.shape[1], e_in.shape[1]
    steps = size // block
    core = flags[1]

    def at(i):
        return slice(i * block, (i + 1) * block)

    def arrival(i, which):
        source = own_d if which == 0 else other_d
        side = core if which == 0 else 1 - core
        columns = pl.ds(pl.multiple_of(side * half, half), half)
        return pltpu.make_async_copy(source.at[at(i), :], given.at[at(i), columns], sems.at[which, i])

    rows, columns = places(block)
    on_diagonal = rows == columns
    identity = jnp.where(on_diagonal, 1.0, 0.0).astype(F32)
    e_copy = pltpu.make_async_copy(e_hbm, e_in, sems.at[2, 0])
    r_copy = pltpu.make_async_copy(r_hbm, r_in, sems.at[2, 1])

    @pl.when(flags[0] == 0)
    def _():
        solved_e[...] = jnp.zeros_like(solved_e)
        solved_r[...] = jnp.zeros_like(solved_r)
        corner_out[...] = jnp.zeros_like(corner_out)
        folded_out[...] = jnp.zeros_like(folded_out)

    @pl.when(flags[0] != 0)
    def _():
        for i in range(steps):
            arrival(i, 0).start()
            arrival(i, 1).start()
        r_copy.start()
        e_copy.start()

        def take(i):
            arrival(i, 0).wait()
            arrival(i, 1).wait()
            diag[at(i), i * block:] = given[at(i), i * block:].astype(F32)

        def take_r():
            r_copy.wait()
            left_r[...] = r_in[...].astype(F32)

        def take_e():
            e_copy.wait()
            left_e[...] = e_in[...].astype(F32)

        take(0)
        result = []
        fillers = [functools.partial(take, i) for i in range(1, steps)] + [take_r, take_e]
        interleave(root_stages(diag[at(0), at(0)], on_diagonal, identity, result), fillers)
        for k in range(steps):
            root, gap_square = result
            near[k:k + 1, :] = jnp.sum(gap_square * gap_square, axis=0, keepdims=True)
            result, part_e, part_r = [], [], []

            def panel(j):
                value = three(nn, root, split(diag[at(k), at(j)]))
                high[:, at(j)], low[:, at(j)] = split(value)
                high_t[at(j), :], low_t[at(j), :] = split(value.T)

            def update(i, j):
                left = (high_t[at(i), :], low_t[at(i), :])
                diag[at(i), at(j)] -= three(nn, left, (high[:, at(j)], low[:, at(j)]))

            def solve_r():
                part_r.extend(split(three(nt, split(left_r[:, at(k)]), root)))
                solved_r[:, at(k)] = part_r[0]

            def update_r(i):
                left_r[:, at(i)] -= three(nn, part_r, (high[:, at(i)], low[:, at(i)]))

            def solve_e():
                value = three(nn, root, split(left_e[at(k), :]))
                part_e.extend(split(value))
                solved_e[at(k), :] = part_e[0]
                turned[:, at(k)] = value.T.astype(BF16)

            def update_e(i):
                left_e[at(i), :] -= three(nn, (high_t[at(i), :], low_t[at(i), :]), part_e)

            fillers = [functools.partial(panel, j) for j in range(k + 2, steps)]
            fillers += [
                functools.partial(update, i, j)
                for i in range(k + 1, steps) for j in range(max(i, k + 2), steps)
            ]
            fillers.append(solve_e)
            fillers += [functools.partial(update_e, i) for i in range(k + 1, steps)]
            fillers.append(solve_r)
            fillers += [functools.partial(update_r, i) for i in range(k + 1, steps)]
            if k + 1 < steps:
                panel(k + 1)
                update(k + 1, k + 1)
                stages = root_stages(diag[at(k + 1), at(k + 1)], on_diagonal, identity, result)
                interleave(stages, fillers)
            else:
                interleave((), fillers)
        worst = jnp.max(jnp.sum(near[0:steps, :], axis=1, keepdims=True))

        @pl.when(jnp.logical_not(worst <= NEAR**4))
        def _():
            for i in range(steps):
                diag[at(i), i * block:] = given[at(i), i * block:].astype(F32)
            left_e[...] = e_in[...].astype(F32)
            left_r[...] = r_in[...].astype(F32)

            def spot(i):
                return pl.ds(pl.multiple_of(i * block, block), block)

            def eliminate(k, carry):
                now = spot(k)
                root = root_until_near(diag[now, now], on_diagonal, identity, unit_ref, root_ref)
                part_r = split(three(nt, split(left_r[:, now]), root))
                solved_r[:, now] = part_r[0]

                value = three(nn, root, split(left_e[now, :]))
                part_e = split(value)
                solved_e[now, :] = part_e[0]
                turned[:, now] = value.T.astype(BF16)

                def panel(j, carry):
                    there = spot(j)
                    value = three(nn, root, split(diag[now, there]))
                    high[:, there], low[:, there] = split(value)
                    high_t[there, :], low_t[there, :] = split(value.T)
                    left_r[:, there] -= three(nn, part_r, (high[:, there], low[:, there]))
                    left = (high_t[there, :], low_t[there, :])
                    left_e[there, :] -= three(nn, left, part_e)
                    return carry

                def row(i, carry):
                    here = spot(i)
                    left = (high_t[here, :], low_t[here, :])

                    def update(j, carry):
                        there = spot(j)
                        diag[here, there] -= three(nn, left, (high[:, there], low[:, there]))
                        return carry

                    return lax.fori_loop(i, steps, update, carry)

                lax.fori_loop(k + 1, steps, panel, 0)
                lax.fori_loop(k + 1, steps, row, 0)
                return carry

            lax.fori_loop(0, steps, eliminate, 0)

        corner = width // 2
        first = nn(turned[0:corner, :], solved_e[:, 0:corner])
        second = nn(turned[corner:width, :], solved_e[:, corner:width])
        folded, diagonal = fold(first, second, places(corner))
        folded_out[0:corner, :] = folded.astype(BF16)
        folded_out[corner:, :] = jnp.broadcast_to(diagonal, (PAD, corner)).astype(BF16)
        corner_out[...] = nn(turned[0:corner, :], solved_e[:, corner:width]).astype(BF16)


def fold(first, second, strict):
    rows, columns = strict
    return jnp.where(rows <= columns, first, second), diagonal_row(second, rows == columns)


def unfold(folded, diagonal, strict):
    rows, columns = strict
    turned = folded.T
    first = jnp.where(rows <= columns, folded, turned)
    second = jnp.where(rows > columns, folded, jnp.where(rows < columns, turned, diagonal))
    return first, second


ANY = pl.BlockSpec(memory_space=pl.ANY)
VMEM = pl.BlockSpec(memory_space=pltpu.VMEM)
SMEM = pl.BlockSpec(memory_space=pltpu.SMEM)


def cost(flops, bytes_accessed):
    return pl.CostEstimate(flops=flops, bytes_accessed=bytes_accessed, transcendentals=0)


def params(mib):
    return pltpu.CompilerParams(vmem_limit_bytes=mib * 2**20)


def eliminate(flags, own_d, other_d, e, r):
    size, block = own_d.shape[0], BLOCK
    width = e.shape[1]
    return pl.pallas_call(
        eliminate_kernel,
        out_shape=(
            jax.ShapeDtypeStruct(e.shape, BF16),
            jax.ShapeDtypeStruct(r.shape, BF16),
            jax.ShapeDtypeStruct((width // 2, width // 2), BF16),
            jax.ShapeDtypeStruct((width // 2 + PAD, width // 2), BF16),
        ),
        in_specs=[SMEM, ANY, VMEM, ANY, ANY],
        out_specs=(VMEM, VMEM, VMEM, VMEM),
        scratch_shapes=[
            pltpu.VMEM((size, size), BF16),
            pltpu.VMEM((size, size), F32),
            pltpu.VMEM(e.shape, BF16),
            pltpu.VMEM(r.shape, BF16),
            pltpu.VMEM(e.shape, F32),
            pltpu.VMEM(r.shape, F32),
            pltpu.VMEM((block, size), BF16),
            pltpu.VMEM((block, size), BF16),
            pltpu.VMEM((size, block), BF16),
            pltpu.VMEM((size, block), BF16),
            pltpu.VMEM((width, size), BF16),
            pltpu.VMEM((-(-(size // block) // 8) * 8, block), F32),
            pltpu.VMEM((block, block), F32),
            pltpu.VMEM((block, block), F32),
            pltpu.SemaphoreType.DMA((3, size // block)),
        ],
        compiler_params=params(52),
        cost_estimate=cost(28 * 10**9, 16 * 2**20),
    )(flags, own_d, other_d, e, r)


def tip_kernel(flags, own_r, other_r, out):
    width = own_r.shape[0]

    @pl.when(flags[0] == 0)
    def _():
        out[...] = jnp.zeros_like(out)

    @pl.when(jnp.logical_and(flags[0] != 0, flags[1] == 0))
    def _():
        out[0:width, :] = nt(own_r[...], other_r[...]).astype(BF16)
        out[width:, :] = jnp.zeros((out.shape[0] - width, width), BF16)

    @pl.when(jnp.logical_and(flags[0] != 0, flags[1] != 0))
    def _():
        first = nt(other_r[...], other_r[...])
        second = nt(own_r[...], own_r[...])
        folded, diagonal = fold(first, second, places(width))
        out[0:width, :] = folded.astype(BF16)
        out[width:, :] = jnp.broadcast_to(diagonal, (out.shape[0] - width, width)).astype(BF16)


def tip_term(flags, own_r, other_r):
    width = own_r.shape[0]
    return pl.pallas_call(
        tip_kernel,
        out_shape=jax.ShapeDtypeStruct((width + PAD, width), BF16),
        in_specs=[SMEM, VMEM, VMEM],
        out_specs=VMEM,
        compiler_params=params(16),
        cost_estimate=cost(10**9, 3 * 2**20),
    )(flags, own_r, other_r)


def arrow_kernel(flags, own_r, other_r, own_e, *outs):
    rows = own_r.shape[0]
    share = 2 * rows // len(outs)
    active, core = flags[2], flags[1]

    @pl.when(active == 0)
    def _():
        for out in outs:
            out[...] = jnp.zeros_like(out)

    def write(first, second):
        for source, base in ((first, 0), (second, rows)):
            value = (-nn(source[...], own_e[...])).astype(BF16)
            for i, out in enumerate(outs):
                low, high = max(base, i * share), min(base + rows, (i + 1) * share)
                if low < high:
                    out[low - i * share:high - i * share, :] = value[low - base:high - base, :]

    @pl.when(jnp.logical_and(active != 0, core == 0))
    def _():
        write(own_r, other_r)

    @pl.when(jnp.logical_and(active != 0, core != 0))
    def _():
        write(other_r, own_r)


def arrow_terms(flags, own_r, other_r, own_e):
    piece = jax.ShapeDtypeStruct((2 * own_r.shape[0] // PIECES, own_e.shape[1]), BF16)
    return pl.pallas_call(
        arrow_kernel,
        out_shape=(piece,) * PIECES,
        in_specs=[SMEM, VMEM, VMEM, VMEM],
        out_specs=(VMEM,) * PIECES,
        compiler_params=params(24),
        cost_estimate=cost(2 * 10**9, 6 * 2**20),
    )(flags, own_r, other_r, own_e)


def cross_kernel(flags, own_e, other_e, out):
    width = own_e.shape[1]
    half = width // 2

    @pl.when(flags[2] == 0)
    def _():
        out[...] = jnp.zeros_like(out)

    @pl.when(jnp.logical_and(flags[2] != 0, flags[1] == 0))
    def _():
        out[...] = nn(other_e[:, 0:half].T, own_e[...]).astype(BF16)

    @pl.when(jnp.logical_and(flags[2] != 0, flags[1] != 0))
    def _():
        out[...] = nn(own_e[:, half:width].T, other_e[...]).astype(BF16)


def cross_term(flags, own_e, other_e):
    width = own_e.shape[1]
    return pl.pallas_call(
        cross_kernel,
        out_shape=jax.ShapeDtypeStruct((width // 2, width), BF16),
        in_specs=[SMEM, VMEM, VMEM],
        out_specs=VMEM,
        compiler_params=params(24),
        cost_estimate=cost(2 * 10**9, 6 * 2**20),
    )(flags, own_e, other_e)


def separator_kernel(flags, separator, corner_in, folded, own_cross, other_cross, out):
    width = separator.shape[1]
    half = width // 2
    core = flags[1]
    first, second = unfold(
        folded[0:half, :].astype(F32), folded[half:half + 1, :].astype(F32), places(half)
    )
    corner = corner_in[...].astype(F32)
    base = pl.multiple_of(core * width, width)

    def less(rows, columns, term):
        out[rows, columns] = (separator[rows, columns].astype(F32) - term).astype(BF16)

    top, bottom = pl.ds(base, half), pl.ds(base + half, half)
    left, right = slice(0, half), slice(half, width)
    less(top, left, first)
    less(top, right, corner)
    less(bottom, left, corner.T)
    less(bottom, right, second)

    @pl.when(core == 0)
    def _():
        less(slice(width, width + half), slice(0, width), own_cross[...].astype(F32))
        less(slice(width + half, 2 * width), slice(0, width), other_cross[...].astype(F32))

    @pl.when(core != 0)
    def _():
        less(slice(0, width), left, other_cross[...].astype(F32).T)
        less(slice(0, width), right, own_cross[...].astype(F32).T)


def separator_less(flags, separator, corner, folded, own_cross, other_cross):
    return pl.pallas_call(
        separator_kernel,
        out_shape=jax.ShapeDtypeStruct(separator.shape, BF16),
        in_specs=[SMEM] + [VMEM] * 5,
        out_specs=VMEM,
        compiler_params=params(24),
        cost_estimate=cost(10**6, 6 * 2**20),
    )(flags, separator, corner, folded, own_cross, other_cross)


def new_tip_kernel(flags, tip, own_sum, other_sum, out):
    width = tip.shape[1]
    core = flags[1]

    @pl.when(core == 0)
    def _():
        first, _ = unfold(
            other_sum[0:width, :].astype(F32), other_sum[width:width + 1, :].astype(F32), places(width)
        )
        out[0:width, :] = tip[0:width, :].astype(F32) - first
        out[width:, :] = tip[width:, :].astype(F32) - own_sum[0:width, :].astype(F32).T

    @pl.when(core != 0)
    def _():
        _, second = unfold(
            own_sum[0:width, :].astype(F32), own_sum[width:width + 1, :].astype(F32), places(width)
        )
        out[0:width, :] = tip[0:width, :].astype(F32) - other_sum[0:width, :].astype(F32)
        out[width:, :] = tip[width:, :].astype(F32) - second


def tip_less(flags, tip, own_sum, other_sum):
    return pl.pallas_call(
        new_tip_kernel,
        out_shape=jax.ShapeDtypeStruct(tip.shape, F32),
        in_specs=[SMEM, VMEM, VMEM, VMEM],
        out_specs=VMEM,
        compiler_params=params(16),
        cost_estimate=cost(10**6, 3 * 2**20),
    )(flags, tip, own_sum, other_sum)


def swapped(x):
    return lax.ppermute(x, "space", [(0, 1), (1, 0)])


def to_previous(x):
    count = lax.axis_size("tm")
    return lax.ppermute(x, "tm", [(i, i - 1) for i in range(1, count)])


def added(*terms):
    return sum(term.astype(F32) for term in terms).astype(BF16)


def summed(term):
    count = lax.axis_size("tm")
    term = added(term, lax.ppermute(term, "tm", [(i, i + 1) for i in range(0, count, 2)]))
    distance = 2
    while distance < count:
        pairs = [(i, i ^ distance) for i in range(1, count, 2)]
        term = added(term, lax.ppermute(term, "tm", pairs))
        distance *= 2
    returned = lax.ppermute(term, "tm", [(i + 1, i) for i in range(0, count, 2)])
    return jnp.where(lax.axis_index("tm") % 2 == 0, returned, term)


def on_device(interior_diag, coupling, arrow_rows, separator_diag, tip, lengths):
    position = lax.axis_index("tm")
    active = lengths[position] == 2
    flags = jnp.stack(
        [active, lax.axis_index("space") != 0, jnp.logical_and(active, position != 0)]
    ).astype(jnp.int32)
    other_diag = swapped(interior_diag)
    own_e, own_r, corner, folded = eliminate(flags, interior_diag, other_diag, coupling, arrow_rows)
    corner = to_previous(corner)
    other_r = swapped(own_r)
    term = tip_term(flags, own_r, other_r)
    tip_sum = summed(term)
    folded = to_previous(folded)
    other_e = swapped(own_e)
    cross = cross_term(flags, own_e, other_e)
    cross = to_previous(cross)
    pieces = arrow_terms(flags, own_r, other_r, own_e)
    received = []
    for piece in pieces:
        received.append(to_previous(piece))
    other_cross = swapped(cross)
    new_separator = separator_less(flags, separator_diag, corner, folded, cross, other_cross)
    other_sum = swapped(tip_sum)
    new_tip = tip_less(flags, tip, tip_sum, other_sum)
    arrow_fill = jnp.concatenate(received, axis=0)
    return (new_separator, arrow_fill, new_tip)


def solution(mesh):
    return jax.shard_map(
        on_device,
        mesh=mesh,
        in_specs=(
            P(("groups", "tm"), "space"),
            P(("groups", "tm"), "space"),
            P(("groups", "tm", "space"), None),
            P(("groups", "tm"), "space"),
            P("groups", "space"),
            P("groups"),
        ),
        out_specs=(
            P(("groups", "tm"), "space"),
            P(("groups", "tm"), "space"),
            P("groups", "space"),
        ),
        check_vma=False,
    )
```

profile of v0, /device:TPU:0, one launch (start us, length us, event | category | flops | bytes accessed | tf_op | source)
XLA Modules:
  0.0 132.0 jit_solution(17918453905378774595)
XLA Ops:
  0.6 0.6 collective-permute-start
  1.2 1.2 dynamic_slice.3
  3.2 2.5 %collective-permute-done.other_d = bf16[1536,768]{1,0:T(8,128)(2,1)} collective-permute-done((bf16[1536,768]{1,0:T(8,128)(2,1)}, bf16[1536,768]{1,0:T(8,128)(2,1)}, u32[]{:S(2)}, u32[]{:S(2)}) %collective-permute-start) | collective-permute-done | bytes 2359328 | tf_op jit(solution)/shard_map/ppermute | solution.py:522
  5.7 28.8 %shard_map.85 = (bf16[1536,768]{1,0:T(8,128)(2,1)}, bf16[384,1536]{1,0:T(8,128)(2,1)S(1)}, bf16[384,384]{1,0:T(8,128)(2,1)S(1)}, bf16[400,384]{1,0:T(8,128)(2,1)S(1)}) custom-call(s32[3]{0:T(128)S(1)} %add_convert_fusion.3.flags, bf16[1536,768]{1,0:T(8,128)(2,1)} %own_d.1, bf16[1536,768]{1,0:T(8,128)(2,1)} %collective-permute-done.other_d, ...), custom_call_target="tpu_custom_call" | custom-call | flops 28000000000 | bytes 16777216 | tf_op jit(solution)/shard_map/pallas_call | solution.py:314
  34.5 0.4 collective-permute-start.6
  34.9 0.1 collective-permute-start.3
  35.0 2.3 %collective-permute-done.6.other_r = bf16[384,1536]{1,0:T(8,128)(2,1)S(1)} collective-permute-done((bf16[384,1536]{1,0:T(8,128)(2,1)S(1)}, bf16[384,1536]{1,0:T(8,128)(2,1)S(1)}, u32[]{:S(2)}, u32[]{:S(2)}) %collective-permute-start.6) | collective-permute-done | bytes 1179680 | tf_op jit(solution)/shard_map/ppermute | solution.py:522
  37.4 1.3 %shard_map.89 = bf16[400,384]{1,0:T(8,128)(2,1)S(1)} custom-call(s32[3]{0:T(128)S(1)} %add_convert_fusion.3.flags, bf16[384,1536]{1,0:T(8,128)(2,1)S(1)} %get-tuple-element.13.own_r, bf16[384,1536]{1,0:T(8,128)(2,1)S(1)} %collective-permute-done.6.other_r), custom_call_target="tpu_custom_call" | custom-call | flops 1000000000 | bytes 3145728 | tf_op jit(solution)/shard_map/pallas_call | solution.py:369
  38.7 1.3 collective-permute-start.10
  40.0 7.3 %collective-permute-done.10 = bf16[400,384]{1,0:T(8,128)(2,1)S(1)} collective-permute-done((bf16[400,384]{1,0:T(8,128)(2,1)S(1)}, bf16[400,384]{1,0:T(8,128)(2,1)S(1)}, u32[]{:S(2)}, u32[]{:S(2)}) %collective-permute-start.10) | collective-permute-done | bytes 307232 | tf_op jit(solution)/shard_map/ppermute | solution.py:536
  47.5 0.7 collective-permute-start.11
  48.2 0.7 collective-permute-start.12
  48.9 0.6 shard_map.86
  49.6 1.3 collective-permute-start.4
  50.9 0.8 add_convert_fusion
  51.7 1.3 collective-permute-start.13
  53.0 0.6 shard_map.88
  53.6 1.4 %collective-permute-start.9 = (bf16[256,768]{1,0:T(8,128)(2,1)S(1)}, bf16[256,768]{1,0:T(8,128)(2,1)}, u32[]{:S(2)}, u32[]{:S(2)}) collective-permute-start(bf16[256,768]{1,0:T(8,128)(2,1)S(1)} %get-tuple-element.16), channel_id=1, source_target_pairs={{2,0},{4,2},{6,4},{8,6},{10,8},{12,10},{14,12},{3,1},{5,3},{7,5},{... | collective-permute-start | bytes 1179656 | tf_op jit(solution)/shard_map/ppermute | solution.py:527
  55.0 1.3 collective-permute-start.8
  56.3 27.6 %collective-permute-done.4.own_cross = bf16[384,768]{1,0:T(8,128)(2,1)S(1)} collective-permute-done((bf16[384,768]{1,0:T(8,128)(2,1)S(1)}, bf16[384,768]{1,0:T(8,128)(2,1)S(1)}, u32[]{:S(2)}, u32[]{:S(2)}) %collective-permute-start.4) | collective-permute-done | bytes 589856 | tf_op jit(solution)/shard_map/ppermute | solution.py:527
  83.9 1.3 collective-permute-start.7
  85.2 7.5 %collective-permute-done.13 = bf16[400,384]{1,0:T(8,128)(2,1)} collective-permute-done((bf16[400,384]{1,0:T(8,128)(2,1)}, bf16[400,384]{1,0:T(8,128)(2,1)}, u32[]{:S(2)}, u32[]{:S(2)}) %collective-permute-start.13) | collective-permute-done | bytes 307232 | tf_op jit(solution)/shard_map/ppermute | solution.py:542
  92.7 1.0 broadcast_select_fusion.own_sum
  93.8 7.3 %collective-permute-done.9 = bf16[256,768]{1,0:T(8,128)(2,1)} collective-permute-done((bf16[256,768]{1,0:T(8,128)(2,1)S(1)}, bf16[256,768]{1,0:T(8,128)(2,1)}, u32[]{:S(2)}, u32[]{:S(2)}) %collective-permute-start.9) | collective-permute-done | bytes 393248 | tf_op jit(solution)/shard_map/ppermute | solution.py:527
  101.2 1.3 collective-permute-start.2
  102.5 7.1 %collective-permute-done.8 = bf16[256,768]{1,0:T(8,128)(2,1)} collective-permute-done((bf16[256,768]{1,0:T(8,128)(2,1)S(1)}, bf16[256,768]{1,0:T(8,128)(2,1)}, u32[]{:S(2)}, u32[]{:S(2)}) %collective-permute-start.8) | collective-permute-done | bytes 393248 | tf_op jit(solution)/shard_map/ppermute | solution.py:527
  109.6 1.4 %collective-permute-start.1 = (bf16[384,384]{1,0:T(8,128)(2,1)S(1)}, bf16[384,384]{1,0:T(8,128)(2,1)S(1)}, u32[]{:S(2)}, u32[]{:S(2)}) collective-permute-start(bf16[384,384]{1,0:T(8,128)(2,1)S(1)} %get-tuple-element.10), channel_id=1, source_target_pairs={{2,0},{4,2},{6,4},{8,6},{10,8},{12,10},{14,12},{3,1},{5,3},{7,5},{... | collective-permute-start | bytes 884744 | tf_op jit(solution)/shard_map/ppermute | solution.py:527
  111.0 6.9 %collective-permute-done.7 = bf16[256,768]{1,0:T(8,128)(2,1)S(1)} collective-permute-done((bf16[256,768]{1,0:T(8,128)(2,1)S(1)}, bf16[256,768]{1,0:T(8,128)(2,1)S(1)}, u32[]{:S(2)}, u32[]{:S(2)}) %collective-permute-start.7) | collective-permute-done | bytes 393248 | tf_op jit(solution)/shard_map/ppermute | solution.py:527
  117.9 2.2 %pad_maximum_fusion = bf16[768,768]{1,0:T(8,128)(2,1)} fusion(bf16[256,768]{1,0:T(8,128)(2,1)} %collective-permute-done.9, bf16[256,768]{1,0:T(8,128)(2,1)} %collective-permute-done.8, bf16[256,768]{1,0:T(8,128)(2,1)S(1)} %collective-permute-done.7), kind=kLoop, calls=%fused_computation | loop fusion | flops 3538944 | bytes 2359296 | tf_op jit(solution)/shard_map/concatenate | solution.py:570
  120.1 1.8 %shard_map.90 = f32[768,384]{1,0:T(8,128)} custom-call(s32[3]{0:T(128)S(1)} %add_convert_fusion.3.flags, bf16[768,384]{1,0:T(8,128)(2,1)S(1)} %copy-done.1, bf16[400,384]{1,0:T(8,128)(2,1)S(1)} %broadcast_select_fusion.own_sum, bf16[400,384]{1,0:T(8,128)(2,1)S(1)} %collective-permute-done.14.other_sum), custom_call_target="tpu_custom_call" | custom-call | flops 1000000 | bytes 3145728 | tf_op jit(solution)/shard_map/pallas_call | solution.py:511
  121.9 7.3 %collective-permute-done.1.corner_in = bf16[384,384]{1,0:T(8,128)(2,1)S(1)} collective-permute-done((bf16[384,384]{1,0:T(8,128)(2,1)S(1)}, bf16[384,384]{1,0:T(8,128)(2,1)S(1)}, u32[]{:S(2)}, u32[]{:S(2)}) %collective-permute-start.1) | collective-permute-done | bytes 294944 | tf_op jit(solution)/shard_map/ppermute | solution.py:527
  129.3 2.7 %shard_map.87 = bf16[1536,768]{1,0:T(8,128)(2,1)} custom-call(s32[3]{0:T(128)S(1)} %add_convert_fusion.3.flags, bf16[1536,768]{1,0:T(8,128)(2,1)S(1)} %copy-done, bf16[384,384]{1,0:T(8,128)(2,1)S(1)} %collective-permute-done.1.corner_in, bf16[400,384]{1,0:T(8,128)(2,1)S(1)} %collective-permute-done.2.folded, ...), custom_call_target="tpu_custom_call" | custom-call | flops 1000000 | bytes 6291456 | tf_op jit(solution)/shard_map/pallas_call | solution.py:479
  (17 shorter events, 0.3 us)
Async XLA Ops:
  0.6 5.1 %collective-permute-start = (bf16[1536,768]{1,0:T(8,128)(2,1)}, bf16[1536,768]{1,0:T(8,128)(2,1)}, u32[]{:S(2)}, u32[]{:S(2)}) collective-permute-start(bf16[1536,768]{1,0:T(8,128)(2,1)} %own_d.1), channel_id=1, source_target_pairs={{0,1},{1,0},{2,3},{3,2},{4,5},{5,4},{6,7},{7,6},{8,9},{9,8},{10,11... | collective-permute-start | bytes 7077896 | tf_op jit(solution)/shard_map/ppermute | solution.py:522
  34.5 2.9 %collective-permute-start.6 = (bf16[384,1536]{1,0:T(8,128)(2,1)S(1)}, bf16[384,1536]{1,0:T(8,128)(2,1)S(1)}, u32[]{:S(2)}, u32[]{:S(2)}) collective-permute-start(bf16[384,1536]{1,0:T(8,128)(2,1)S(1)} %get-tuple-element.13.own_r), channel_id=1, source_target_pairs={{0,1},{1,0},{2,3},{3,2},{4,5},{5,4},{6,7},{7,6},{8,9},{9,8},{10,11... | collective-permute-start | bytes 3538952 | tf_op jit(solution)/shard_map/ppermute | solution.py:522
  34.9 14.0 %copy-start.2 = (bf16[1536,768]{1,0:T(8,128)(2,1)S(1)}, bf16[1536,768]{1,0:T(8,128)(2,1)}, u32[]{:S(2)}) copy-start(bf16[1536,768]{1,0:T(8,128)(2,1)} %get-tuple-element.12.own_e) | copy-start | bytes 7077892
  34.9 14.0 %collective-permute-start.3 = (bf16[1536,768]{1,0:T(8,128)(2,1)}, bf16[1536,768]{1,0:T(8,128)(2,1)S(1)}, u32[]{:S(2)}, u32[]{:S(2)}) collective-permute-start(bf16[1536,768]{1,0:T(8,128)(2,1)} %get-tuple-element.12.own_e), channel_id=1, source_target_pairs={{0,1},{1,0},{2,3},{3,2},{4,5},{5,4},{6,7},{7,6},{8,9},{9,8},{10,11... | collective-permute-start | bytes 7077896 | tf_op jit(solution)/shard_map/ppermute | solution.py:522
  38.7 8.6 %collective-permute-start.10 = (bf16[400,384]{1,0:T(8,128)(2,1)S(1)}, bf16[400,384]{1,0:T(8,128)(2,1)S(1)}, u32[]{:S(2)}, u32[]{:S(2)}) collective-permute-start(bf16[400,384]{1,0:T(8,128)(2,1)S(1)} %shard_map.89), channel_id=1, source_target_pairs={{0,2},{4,6},{8,10},{12,14},{1,3},{5,7},{9,11},{13,15},{16,18},{20,... | collective-permute-start | bytes 921608 | tf_op jit(solution)/shard_map/ppermute | solution.py:536
  47.5 0.7 collective-permute-start.11
  48.2 2.6 %collective-permute-start.12 = (bf16[400,384]{1,0:T(8,128)(2,1)S(1)}, bf16[400,384]{1,0:T(8,128)(2,1)S(1)}, u32[]{:S(2)}, u32[]{:S(2)}) collective-permute-start(bf16[400,384]{1,0:T(8,128)(2,1)S(1)} %add_convert_fusion.1), channel_id=1, source_target_pairs={{2,10},{6,14},{10,2},{14,6},{3,11},{7,15},{11,3},{15,7},{18,26},{2... | collective-permute-start | bytes 921608 | tf_op jit(solution)/shard_map/ppermute | solution.py:540
  49.6 34.4 %collective-permute-start.4 = (bf16[384,768]{1,0:T(8,128)(2,1)S(1)}, bf16[384,768]{1,0:T(8,128)(2,1)S(1)}, u32[]{:S(2)}, u32[]{:S(2)}) collective-permute-start(bf16[384,768]{1,0:T(8,128)(2,1)S(1)} %shard_map.86), channel_id=1, source_target_pairs={{2,0},{4,2},{6,4},{8,6},{10,8},{12,10},{14,12},{3,1},{5,3},{7,5},{... | collective-permute-start | bytes 1769480 | tf_op jit(solution)/shard_map/ppermute | solution.py:527
  51.7 41.1 %collective-permute-start.13 = (bf16[400,384]{1,0:T(8,128)(2,1)}, bf16[400,384]{1,0:T(8,128)(2,1)}, u32[]{:S(2)}, u32[]{:S(2)}) collective-permute-start(bf16[400,384]{1,0:T(8,128)(2,1)} %add_convert_fusion), channel_id=1, source_target_pairs={{2,0},{6,4},{10,8},{14,12},{3,1},{7,5},{11,9},{15,13},{18,16},{22,... | collective-permute-start | bytes 921608 | tf_op jit(solution)/shard_map/ppermute | solution.py:542
  53.6 66.5 %copy-start.1 = (bf16[768,384]{1,0:T(8,128)(2,1)S(1)}, bf16[768,384]{1,0:T(8,128)(2,1)}, u32[]{:S(2)}) copy-start(bf16[768,384]{1,0:T(8,128)(2,1)} %tip.1) | copy-start | bytes 1769476
  53.6 47.6 %collective-permute-start.9 = (bf16[256,768]{1,0:T(8,128)(2,1)S(1)}, bf16[256,768]{1,0:T(8,128)(2,1)}, u32[]{:S(2)}, u32[]{:S(2)}) collective-permute-start(bf16[256,768]{1,0:T(8,128)(2,1)S(1)} %get-tuple-element.16), channel_id=1, source_target_pairs={{2,0},{4,2},{6,4},{8,6},{10,8},{12,10},{14,12},{3,1},{5,3},{7,5},{... | collective-permute-start | bytes 1179656 | tf_op jit(solution)/shard_map/ppermute | solution.py:527
  55.0 54.5 %collective-permute-start.8 = (bf16[256,768]{1,0:T(8,128)(2,1)S(1)}, bf16[256,768]{1,0:T(8,128)(2,1)}, u32[]{:S(2)}, u32[]{:S(2)}) collective-permute-start(bf16[256,768]{1,0:T(8,128)(2,1)S(1)} %get-tuple-element.15), channel_id=1, source_target_pairs={{2,0},{4,2},{6,4},{8,6},{10,8},{12,10},{14,12},{3,1},{5,3},{7,5},{... | collective-permute-start | bytes 1179656 | tf_op jit(solution)/shard_map/ppermute | solution.py:527
  83.9 45.3 %collective-permute-start.5 = (bf16[384,768]{1,0:T(8,128)(2,1)S(1)}, bf16[384,768]{1,0:T(8,128)(2,1)S(1)}, u32[]{:S(2)}, u32[]{:S(2)}) collective-permute-start(bf16[384,768]{1,0:T(8,128)(2,1)S(1)} %collective-permute-done.4.own_cross), channel_id=1, source_target_pairs={{0,1},{1,0},{2,3},{3,2},{4,5},{5,4},{6,7},{7,6},{8,9},{9,8},{10,11... | collective-permute-start | bytes 1769480 | tf_op jit(solution)/shard_map/ppermute | solution.py:522
  83.9 34.0 %collective-permute-start.7 = (bf16[256,768]{1,0:T(8,128)(2,1)S(1)}, bf16[256,768]{1,0:T(8,128)(2,1)S(1)}, u32[]{:S(2)}, u32[]{:S(2)}) collective-permute-start(bf16[256,768]{1,0:T(8,128)(2,1)S(1)} %get-tuple-element.14), channel_id=1, source_target_pairs={{2,0},{4,2},{6,4},{8,6},{10,8},{12,10},{14,12},{3,1},{5,3},{7,5},{... | collective-permute-start | bytes 1179656 | tf_op jit(solution)/shard_map/ppermute | solution.py:527
  93.7 26.4 %collective-permute-start.14 = (bf16[400,384]{1,0:T(8,128)(2,1)S(1)}, bf16[400,384]{1,0:T(8,128)(2,1)S(1)}, u32[]{:S(2)}, u32[]{:S(2)}) collective-permute-start(bf16[400,384]{1,0:T(8,128)(2,1)S(1)} %broadcast_select_fusion.own_sum), channel_id=1, source_target_pairs={{0,1},{1,0},{2,3},{3,2},{4,5},{5,4},{6,7},{7,6},{8,9},{9,8},{10,11... | collective-permute-start | bytes 921608 | tf_op jit(solution)/shard_map/ppermute | solution.py:522
  101.2 28.1 %collective-permute-start.2 = (bf16[400,384]{1,0:T(8,128)(2,1)S(1)}, bf16[400,384]{1,0:T(8,128)(2,1)S(1)}, u32[]{:S(2)}, u32[]{:S(2)}) collective-permute-start(bf16[400,384]{1,0:T(8,128)(2,1)S(1)} %get-tuple-element.11), channel_id=1, source_target_pairs={{2,0},{4,2},{6,4},{8,6},{10,8},{12,10},{14,12},{3,1},{5,3},{7,5},{... | collective-permute-start | bytes 921608 | tf_op jit(solution)/shard_map/ppermute | solution.py:527
  109.6 19.7 %copy-start = (bf16[1536,768]{1,0:T(8,128)(2,1)S(1)}, bf16[1536,768]{1,0:T(8,128)(2,1)}, u32[]{:S(2)}) copy-start(bf16[1536,768]{1,0:T(8,128)(2,1)} %separator.1) | copy-start | bytes 7077892
  109.6 19.7 %collective-permute-start.1 = (bf16[384,384]{1,0:T(8,128)(2,1)S(1)}, bf16[384,384]{1,0:T(8,128)(2,1)S(1)}, u32[]{:S(2)}, u32[]{:S(2)}) collective-permute-start(bf16[384,384]{1,0:T(8,128)(2,1)S(1)} %get-tuple-element.10), channel_id=1, source_target_pairs={{2,0},{4,2},{6,4},{8,6},{10,8},{12,10},{14,12},{3,1},{5,3},{7,5},{... | collective-permute-start | bytes 884744 | tf_op jit(solution)/shard_map/ppermute | solution.py:527
where the time goes:
time: 132 us
  waiting for transfers between devices  76 us (58%)
  Pallas kernels  35.8 us (27%)
  starting transfers between devices  13.1 us (10%)
  other arithmetic  4.24 us (3%)
  between operations  1.47 us (1%)
    ppermute x6, waiting for transfers between devices, to_previous(): return lax.ppermute(x, 'tm', [(i, i - 1) for i in range(1, count)])  56.3 us
    pallas_call x1, Pallas kernels, eliminate(): pl.pallas_call(eliminate_kernel, out_shape=(jax.ShapeDtypeStruct(e.shape,...  28.8 us
    ppermute x6, starting transfers between devices, to_previous(): return lax.ppermute(x, 'tm', [(i, i - 1) for i in range(1, count)])  7.98 us
    ppermute x1, waiting for transfers between devices, summed(): lax.ppermute(term, 'tm', [(i + 1, i) for i in range(0, count, 2)])  7.52 us
    ppermute x1, waiting for transfers between devices, summed(): lax.ppermute(term, 'tm', [(i, i + 1) for i in range(0, count, 2)])  7.33 us
    ppermute x5, waiting for transfers between devices, swapped(): return lax.ppermute(x, 'space', [(0, 1), (1, 0)])  4.88 us
    pallas_call x1, Pallas kernels, separator_less(): pl.pallas_call(separator_kernel, out_shape=jax.ShapeDtypeStruct(separator...  2.69 us
  transfers between devices with their start and end apart: 15, of which 9 were waited for; matrix products, arithmetic and copies ran while one was open for 4% of the time, Pallas kernels for 3%

commit v1 on v0

--- a/solution.py
+++ b/solution.py
@@ -319,7 +319,7 @@
             jax.ShapeDtypeStruct((width // 2, width // 2), BF16),
             jax.ShapeDtypeStruct((width // 2 + PAD, width // 2), BF16),
         ),
-        in_specs=[SMEM, ANY, VMEM, ANY, ANY],
+        in_specs=[SMEM, ANY, ANY, ANY, ANY],
         out_specs=(VMEM, VMEM, VMEM, VMEM),
         scratch_shapes=[
             pltpu.VMEM((size, size), BF16),
@@ -518,6 +518,50 @@
     )(flags, tip, own_sum, other_sum)
 
 
+def rows_kernel(count, flags, *refs):
+    sources, out, sem = refs[:count], refs[-2], refs[-1]
+    share = sources[0].shape[0]
+
+    def copy(source, i):
+        place = out.at[i * share:(i + 1) * share, :]
+        return pltpu.make_async_copy(source, place, sem.at[i])
+
+    if count == 1:
+        last = out.shape[0] // share - 1
+        copy(sources[0], last).start()
+        copy(sources[0], last).wait()
+        return
+
+    @pl.when(flags[3] == 0)
+    def _():
+        copy(sources[0], 0).start()
+
+    @pl.when(flags[3] != 0)
+    def _():
+        copy(sources[1], 0).start()
+
+    for i, source in enumerate(sources[2:]):
+        copy(source, i + 1).start()
+    for i, source in enumerate(sources[1:]):
+        copy(source, i).wait()
+
+
+def rows_placed(flags, pieces, whole):
+    count = len(pieces)
+    shape = whole if isinstance(whole, tuple) else whole.shape
+    more = () if isinstance(whole, tuple) else (whole,)
+    return pl.pallas_call(
+        functools.partial(rows_kernel, count),
+        out_shape=jax.ShapeDtypeStruct(shape, BF16),
+        in_specs=[SMEM] + [VMEM] * count + [ANY] * len(more),
+        out_specs=ANY,
+        scratch_shapes=[pltpu.SemaphoreType.DMA((PIECES,))],
+        input_output_aliases={count + 1: 0} if more else {},
+        compiler_params=params(16),
+        cost_estimate=cost(10**6, 2 * 2**20),
+    )(flags, *pieces, *more)
+
+
 def swapped(x):
     return lax.ppermute(x, "space", [(0, 1), (1, 0)])
 
@@ -525,6 +569,11 @@
 def to_previous(x):
     count = lax.axis_size("tm")
     return lax.ppermute(x, "tm", [(i, i - 1) for i in range(1, count)])
+
+
+def from_every_other(x, first):
+    count = lax.axis_size("tm")
+    return lax.ppermute(x, "tm", [(i, i - 1) for i in range(first, count, 2)])
 
 
 def added(*terms):
@@ -547,7 +596,12 @@
     position = lax.axis_index("tm")
     active = lengths[position] == 2
     flags = jnp.stack(
-        [active, lax.axis_index("space") != 0, jnp.logical_and(active, position != 0)]
+        [
+            active,
+            lax.axis_index("space") != 0,
+            jnp.logical_and(active, position != 0),
+            position % 2 != 0,
+        ]
     ).astype(jnp.int32)
     other_diag = swapped(interior_diag)
     own_e, own_r, corner, folded = eliminate(flags, interior_diag, other_diag, coupling, arrow_rows)
@@ -560,14 +614,18 @@
     cross = cross_term(flags, own_e, other_e)
     cross = to_previous(cross)
     pieces = arrow_terms(flags, own_r, other_r, own_e)
-    received = []
-    for piece in pieces:
+    received = [from_every_other(pieces[0], 1)]
+    received.append(from_every_other(pieces[0], 2))
+    for piece in pieces[1:]:
         received.append(to_previous(piece))
+    arrow_fill = rows_placed(
+        flags, received[:-1], (2 * own_r.shape[0], own_e.shape[1])
+    )
+    arrow_fill = rows_placed(flags, received[-1:], arrow_fill)
     other_cross = swapped(cross)
     new_separator = separator_less(flags, separator_diag, corner, folded, cross, other_cross)
     other_sum = swapped(tip_sum)
     new_tip = tip_less(flags, tip, tip_sum, other_sum)
-    arrow_fill = jnp.concatenate(received, axis=0)
     return (new_separator, arrow_fill, new_tip)
 
 

time: 132 us -> 134 us (1.015)
  local copies, waits for them, and re-layouts: 1.25 us -> 4.09 us
  other arithmetic: 4.24 us -> 2.05 us
  Pallas kernels: 35.8 us -> 37.8 us
    ppermute x6 -> x5, waiting for transfers between devices: 56.3 us -> 47.9 us  [to_previous(): return lax.ppermute(x, 'tm', [(i, i - 1) for i in range(1, count)])]
    ppermute x0 -> x2, waiting for transfers between devices: none -> 6.02 us  [from_every_other(): return lax.ppermute(x, 'tm', [(i, i - 1) for i in range(first, count, 2)])]
    unnamed x6 -> x12, local copies, waits for them, and re-layouts: 0.01 us -> 2.85 us
    pallas_call x0 -> x2, Pallas kernels: none -> 2.76 us  [rows_placed(): pl.pallas_call(functools.partial(rows_kernel, count), out_shape=jax.Shape...]
    concatenate x1 -> x0, other arithmetic: 2.2 us -> none  [on_device(): arrow_fill = jnp.concatenate(received, axis=0)]
    ppermute x0 -> x2, starting transfers between devices: none -> 1.98 us  [from_every_other(): return lax.ppermute(x, 'tm', [(i, i - 1) for i in range(first, count, 2)])]
    ppermute x6 -> x5, starting transfers between devices: 7.98 us -> 6.56 us  [to_previous(): return lax.ppermute(x, 'tm', [(i, i - 1) for i in range(1, count)])]
  transfers between devices with their start and end apart: 15 -> 16, of which waited for: 9 -> 9; matrix products, arithmetic and copies ran while one was open for 4% -> 2% of each run, Pallas kernels for 3% -> 5%
where the time goes in v1:
time: 134 us
  waiting for transfers between devices  74.8 us (56%)
  Pallas kernels  37.8 us (28%)
  starting transfers between devices  13.6 us (10%)
  local copies, waits for them, and re-layouts  4.09 us (3%)
  other arithmetic  2.05 us (2%)
  between operations  1.51 us (1%)
    ppermute x5, waiting for transfers between devices, to_previous(): return lax.ppermute(x, 'tm', [(i, i - 1) for i in range(1, count)])  47.9 us
    pallas_call x1, Pallas kernels, eliminate(): pl.pallas_call(eliminate_kernel, out_shape=(jax.ShapeDtypeStruct(e.shape,...  28.1 us
    ppermute x1, waiting for transfers between devices, summed(): lax.ppermute(term, 'tm', [(i + 1, i) for i in range(0, count, 2)])  8.81 us
    ppermute x1, waiting for transfers between devices, summed(): lax.ppermute(term, 'tm', [(i, i + 1) for i in range(0, count, 2)])  7.34 us
    ppermute x5, starting transfers between devices, to_previous(): return lax.ppermute(x, 'tm', [(i, i - 1) for i in range(1, count)])  6.56 us
    ppermute x2, waiting for transfers between devices, from_every_other(): return lax.ppermute(x, 'tm', [(i, i - 1) for i in range(first, count, 2)])  6.02 us
    ppermute x5, waiting for transfers between devices, swapped(): return lax.ppermute(x, 'space', [(0, 1), (1, 0)])  4.74 us
    unnamed x12, local copies, waits for them, and re-layouts  2.85 us
  transfers between devices with their start and end apart: 16, of which 9 were waited for; matrix products, arithmetic and copies ran while one was open for 2% of the time, Pallas kernels for 5%

profile of v1, /device:TPU:0, one launch (start us, length us, event | category | flops | bytes accessed | tf_op | source)
XLA Modules:
  0.0 133.8 jit_solution(6595774478946294920)
XLA Ops:
  1.2 1.2 dynamic_slice.3
  3.2 2.4 %collective-permute-done.other_d = bf16[1536,768]{1,0:T(8,128)(2,1)S(1)} collective-permute-done((bf16[1536,768]{1,0:T(8,128)(2,1)}, bf16[1536,768]{1,0:T(8,128)(2,1)S(1)}, u32[]{:S(2)}, u32[]{:S(2)}) %collective-permute-start) | collective-permute-done | bytes 2359328 | tf_op jit(solution)/shard_map/ppermute | solution.py:566
  5.6 1.4 %copy-done.5 = bf16[1536,768]{1,0:T(8,128)(2,1)} copy-done((bf16[1536,768]{1,0:T(8,128)(2,1)}, bf16[1536,768]{1,0:T(8,128)(2,1)S(1)}, u32[]{:S(2)}) %copy-start.5) | copy-done | bytes 2359320
  7.0 28.1 %shard_map.85 = (bf16[1536,768]{1,0:T(8,128)(2,1)}, bf16[384,1536]{1,0:T(8,128)(2,1)S(1)}, bf16[384,384]{1,0:T(8,128)(2,1)S(1)}, bf16[400,384]{1,0:T(8,128)(2,1)S(1)}) custom-call(s32[4]{0:T(128)S(1)} %add_convert_fusion.3.flags, bf16[1536,768]{1,0:T(8,128)(2,1)} %own_d.1, bf16[1536,768]{1,0:T(8,128)(2,1)} %copy-done.5, bf16[1536,768]{1,0:T(8,128)(2,1)} %e_hbm.1, ...), custom_call_target="tpu_custom_call" | custom-call | flops 28000000000 | bytes 16777216 | tf_op jit(solution)/shard_map/pallas_call | solution.py:314
  35.1 0.7 copy-done.3
  35.8 0.7 copy-done.4
  37.0 2.3 %collective-permute-done.6.other_r = bf16[384,1536]{1,0:T(8,128)(2,1)S(1)} collective-permute-done((bf16[384,1536]{1,0:T(8,128)(2,1)S(1)}, bf16[384,1536]{1,0:T(8,128)(2,1)S(1)}, u32[]{:S(2)}, u32[]{:S(2)}) %collective-permute-start.6) | collective-permute-done | bytes 1179680 | tf_op jit(solution)/shard_map/ppermute | solution.py:566
  39.3 1.3 %shard_map.91 = bf16[400,384]{1,0:T(8,128)(2,1)S(1)} custom-call(s32[4]{0:T(128)S(1)} %add_convert_fusion.3.flags, bf16[384,1536]{1,0:T(8,128)(2,1)S(1)} %get-tuple-element.13.own_r, bf16[384,1536]{1,0:T(8,128)(2,1)S(1)} %collective-permute-done.6.other_r), custom_call_target="tpu_custom_call" | custom-call | flops 1000000000 | bytes 3145728 | tf_op jit(solution)/shard_map/pallas_call | solution.py:369
  40.7 1.3 collective-permute-start.11
  42.0 7.3 %collective-permute-done.11 = bf16[400,384]{1,0:T(8,128)(2,1)S(1)} collective-permute-done((bf16[400,384]{1,0:T(8,128)(2,1)S(1)}, bf16[400,384]{1,0:T(8,128)(2,1)S(1)}, u32[]{:S(2)}, u32[]{:S(2)}) %collective-permute-start.11) | collective-permute-done | bytes 307232 | tf_op jit(solution)/shard_map/ppermute | solution.py:585
  49.4 0.7 collective-permute-start.12
  50.2 0.7 collective-permute-start.13
  51.5 1.3 collective-permute-start.4
  52.8 0.8 add_convert_fusion
  53.6 1.3 collective-permute-start.14
  55.6 1.3 collective-permute-start.8
  56.9 0.7 collective-permute-start.9
  57.6 1.3 collective-permute-start.10
  58.9 27.0 %collective-permute-done.4.own_cross = bf16[384,768]{1,0:T(8,128)(2,1)S(1)} collective-permute-done((bf16[384,768]{1,0:T(8,128)(2,1)S(1)}, bf16[384,768]{1,0:T(8,128)(2,1)S(1)}, u32[]{:S(2)}, u32[]{:S(2)}) %collective-permute-start.4) | collective-permute-done | bytes 589856 | tf_op jit(solution)/shard_map/ppermute | solution.py:571
  85.9 8.8 %collective-permute-done.14 = bf16[400,384]{1,0:T(8,128)(2,1)} collective-permute-done((bf16[400,384]{1,0:T(8,128)(2,1)}, bf16[400,384]{1,0:T(8,128)(2,1)}, u32[]{:S(2)}, u32[]{:S(2)}) %collective-permute-start.14) | collective-permute-done | bytes 307232 | tf_op jit(solution)/shard_map/ppermute | solution.py:591
  94.7 1.3 collective-permute-start.7
  96.0 1.0 broadcast_select_fusion.own_sum
  97.0 6.0 %collective-permute-done.8.refs_0_ = bf16[256,768]{1,0:T(8,128)(2,1)S(1)} collective-permute-done((bf16[256,768]{1,0:T(8,128)(2,1)S(1)}, bf16[256,768]{1,0:T(8,128)(2,1)S(1)}, u32[]{:S(2)}, u32[]{:S(2)}) %collective-permute-start.8) | collective-permute-done | bytes 393248 | tf_op jit(solution)/shard_map/ppermute | solution.py:576
  103.0 1.3 collective-permute-start.2
  104.3 7.1 %collective-permute-done.10.refs_2_ = bf16[256,768]{1,0:T(8,128)(2,1)S(1)} collective-permute-done((bf16[256,768]{1,0:T(8,128)(2,1)S(1)}, bf16[256,768]{1,0:T(8,128)(2,1)S(1)}, u32[]{:S(2)}, u32[]{:S(2)}) %collective-permute-start.10) | collective-permute-done | bytes 393248 | tf_op jit(solution)/shard_map/ppermute | solution.py:571
  111.5 1.4 %collective-permute-start.1 = (bf16[384,384]{1,0:T(8,128)(2,1)}, bf16[384,384]{1,0:T(8,128)(2,1)S(1)}, u32[]{:S(2)}, u32[]{:S(2)}) collective-permute-start(bf16[384,384]{1,0:T(8,128)(2,1)} %copy-done.4), channel_id=1, source_target_pairs={{2,0},{4,2},{6,4},{8,6},{10,8},{12,10},{14,12},{3,1},{5,3},{7,5},{... | collective-permute-start | bytes 884744 | tf_op jit(solution)/shard_map/ppermute | solution.py:571
  112.9 1.4 %shard_map.89.refs_1_ = bf16[768,768]{1,0:T(8,128)(2,1)} custom-call(s32[4]{0:T(128)S(1)} %add_convert_fusion.3.flags, bf16[256,768]{1,0:T(8,128)(2,1)S(1)} %collective-permute-done.8.refs_0_, bf16[256,768]{1,0:T(8,128)(2,1)S(1)} %collective-permute-done.9.refs_1_, bf16[256,768]{1,0:T(8,128)(2,1)S(1)} %collective-permute-done.10.refs_2_), custom_call_target="tpu_custom_call" | custom-call | flops 1000000 | bytes 2097152 | tf_op jit(solution)/shard_map/pallas_call | solution.py:553
  114.3 5.5 %collective-permute-done.7.refs_0_ = bf16[256,768]{1,0:T(8,128)(2,1)S(1)} collective-permute-done((bf16[256,768]{1,0:T(8,128)(2,1)S(1)}, bf16[256,768]{1,0:T(8,128)(2,1)S(1)}, u32[]{:S(2)}, u32[]{:S(2)}) %collective-permute-start.7) | collective-permute-done | bytes 393248 | tf_op jit(solution)/shard_map/ppermute | solution.py:571
  119.9 1.3 shard_map.90
  121.2 1.8 %shard_map.92 = f32[768,384]{1,0:T(8,128)} custom-call(s32[4]{0:T(128)S(1)} %add_convert_fusion.3.flags, bf16[768,384]{1,0:T(8,128)(2,1)S(1)} %copy-done.1, bf16[400,384]{1,0:T(8,128)(2,1)S(1)} %broadcast_select_fusion.own_sum, bf16[400,384]{1,0:T(8,128)(2,1)S(1)} %collective-permute-done.15.other_sum), custom_call_target="tpu_custom_call" | custom-call | flops 1000000 | bytes 3145728 | tf_op jit(solution)/shard_map/pallas_call | solution.py:511
  123.0 8.2 %collective-permute-done.1.corner_in = bf16[384,384]{1,0:T(8,128)(2,1)S(1)} collective-permute-done((bf16[384,384]{1,0:T(8,128)(2,1)}, bf16[384,384]{1,0:T(8,128)(2,1)S(1)}, u32[]{:S(2)}, u32[]{:S(2)}) %collective-permute-start.1) | collective-permute-done | bytes 294944 | tf_op jit(solution)/shard_map/ppermute | solution.py:571
  131.2 2.6 %shard_map.87 = bf16[1536,768]{1,0:T(8,128)(2,1)} custom-call(s32[4]{0:T(128)S(1)} %add_convert_fusion.3.flags, bf16[1536,768]{1,0:T(8,128)(2,1)S(1)} %copy-done, bf16[384,384]{1,0:T(8,128)(2,1)S(1)} %collective-permute-done.1.corner_in, bf16[400,384]{1,0:T(8,128)(2,1)S(1)} %collective-permute-done.2.folded, ...), custom_call_target="tpu_custom_call" | custom-call | flops 1000000 | bytes 6291456 | tf_op jit(solution)/shard_map/pallas_call | solution.py:479
  (26 shorter events, 2.6 us)
Async XLA Ops:
  0.6 4.9 %collective-permute-start = (bf16[1536,768]{1,0:T(8,128)(2,1)}, bf16[1536,768]{1,0:T(8,128)(2,1)S(1)}, u32[]{:S(2)}, u32[]{:S(2)}) collective-permute-start(bf16[1536,768]{1,0:T(8,128)(2,1)} %own_d.1), channel_id=1, source_target_pairs={{0,1},{1,0},{2,3},{3,2},{4,5},{5,4},{6,7},{7,6},{8,9},{9,8},{10,11... | collective-permute-start | bytes 7077896 | tf_op jit(solution)/shard_map/ppermute | solution.py:566
  5.6 1.4 %copy-start.5 = (bf16[1536,768]{1,0:T(8,128)(2,1)}, bf16[1536,768]{1,0:T(8,128)(2,1)S(1)}, u32[]{:S(2)}) copy-start(bf16[1536,768]{1,0:T(8,128)(2,1)S(1)} %collective-permute-done.other_d) | copy-start | bytes 7077892
  35.0 0.7 copy-start.3
  35.8 0.7 copy-start.4
  36.5 2.8 %collective-permute-start.6 = (bf16[384,1536]{1,0:T(8,128)(2,1)S(1)}, bf16[384,1536]{1,0:T(8,128)(2,1)S(1)}, u32[]{:S(2)}, u32[]{:S(2)}) collective-permute-start(bf16[384,1536]{1,0:T(8,128)(2,1)S(1)} %get-tuple-element.13.own_r), channel_id=1, source_target_pairs={{0,1},{1,0},{2,3},{3,2},{4,5},{5,4},{6,7},{7,6},{8,9},{9,8},{10,11... | collective-permute-start | bytes 3538952 | tf_op jit(solution)/shard_map/ppermute | solution.py:566
  36.9 14.1 %copy-start.2 = (bf16[1536,768]{1,0:T(8,128)(2,1)S(1)}, bf16[1536,768]{1,0:T(8,128)(2,1)}, u32[]{:S(2)}) copy-start(bf16[1536,768]{1,0:T(8,128)(2,1)} %get-tuple-element.12.own_e) | copy-start | bytes 7077892
  36.9 14.0 %collective-permute-start.3 = (bf16[1536,768]{1,0:T(8,128)(2,1)}, bf16[1536,768]{1,0:T(8,128)(2,1)S(1)}, u32[]{:S(2)}, u32[]{:S(2)}) collective-permute-start(bf16[1536,768]{1,0:T(8,128)(2,1)} %get-tuple-element.12.own_e), channel_id=1, source_target_pairs={{0,1},{1,0},{2,3},{3,2},{4,5},{5,4},{6,7},{7,6},{8,9},{9,8},{10,11... | collective-permute-start | bytes 7077896 | tf_op jit(solution)/shard_map/ppermute | solution.py:566
  40.7 8.7 %collective-permute-start.11 = (bf16[400,384]{1,0:T(8,128)(2,1)S(1)}, bf16[400,384]{1,0:T(8,128)(2,1)S(1)}, u32[]{:S(2)}, u32[]{:S(2)}) collective-permute-start(bf16[400,384]{1,0:T(8,128)(2,1)S(1)} %shard_map.91), channel_id=1, source_target_pairs={{0,2},{4,6},{8,10},{12,14},{1,3},{5,7},{9,11},{13,15},{16,18},{20,... | collective-permute-start | bytes 921608 | tf_op jit(solution)/shard_map/ppermute | solution.py:585
  49.4 0.7 collective-permute-start.12
  50.2 2.6 %collective-permute-start.13 = (bf16[400,384]{1,0:T(8,128)(2,1)S(1)}, bf16[400,384]{1,0:T(8,128)(2,1)S(1)}, u32[]{:S(2)}, u32[]{:S(2)}) collective-permute-start(bf16[400,384]{1,0:T(8,128)(2,1)S(1)} %add_convert_fusion.1), channel_id=1, source_target_pairs={{2,10},{6,14},{10,2},{14,6},{3,11},{7,15},{11,3},{15,7},{18,26},{2... | collective-permute-start | bytes 921608 | tf_op jit(solution)/shard_map/ppermute | solution.py:589
  51.5 34.4 %collective-permute-start.4 = (bf16[384,768]{1,0:T(8,128)(2,1)S(1)}, bf16[384,768]{1,0:T(8,128)(2,1)S(1)}, u32[]{:S(2)}, u32[]{:S(2)}) collective-permute-start(bf16[384,768]{1,0:T(8,128)(2,1)S(1)} %shard_map.86), channel_id=1, source_target_pairs={{2,0},{4,2},{6,4},{8,6},{10,8},{12,10},{14,12},{3,1},{5,3},{7,5},{... | collective-permute-start | bytes 1769480 | tf_op jit(solution)/shard_map/ppermute | solution.py:571
  53.6 41.1 %collective-permute-start.14 = (bf16[400,384]{1,0:T(8,128)(2,1)}, bf16[400,384]{1,0:T(8,128)(2,1)}, u32[]{:S(2)}, u32[]{:S(2)}) collective-permute-start(bf16[400,384]{1,0:T(8,128)(2,1)} %add_convert_fusion), channel_id=1, source_target_pairs={{2,0},{6,4},{10,8},{14,12},{3,1},{7,5},{11,9},{15,13},{18,16},{22,... | collective-permute-start | bytes 921608 | tf_op jit(solution)/shard_map/ppermute | solution.py:591
  55.6 47.5 %collective-permute-start.8 = (bf16[256,768]{1,0:T(8,128)(2,1)S(1)}, bf16[256,768]{1,0:T(8,128)(2,1)S(1)}, u32[]{:S(2)}, u32[]{:S(2)}) collective-permute-start(bf16[256,768]{1,0:T(8,128)(2,1)S(1)} %get-tuple-element.15), channel_id=1, source_target_pairs={{2,0},{6,4},{10,8},{14,12},{3,1},{7,5},{11,9},{15,13},{18,16},{22,... | collective-permute-start | bytes 1179656 | tf_op jit(solution)/shard_map/ppermute | solution.py:576
  56.9 46.2 %collective-permute-start.9 = (bf16[256,768]{1,0:T(8,128)(2,1)S(1)}, bf16[256,768]{1,0:T(8,128)(2,1)S(1)}, u32[]{:S(2)}, u32[]{:S(2)}) collective-permute-start(bf16[256,768]{1,0:T(8,128)(2,1)S(1)} %get-tuple-element.15), channel_id=1, source_target_pairs={{4,2},{8,6},{12,10},{5,3},{9,7},{13,11},{20,18},{24,22},{28,26},{2... | collective-permute-start | bytes 1179656 | tf_op jit(solution)/shard_map/ppermute | solution.py:576
  57.6 53.9 %collective-permute-start.10 = (bf16[256,768]{1,0:T(8,128)(2,1)S(1)}, bf16[256,768]{1,0:T(8,128)(2,1)S(1)}, u32[]{:S(2)}, u32[]{:S(2)}) collective-permute-start(bf16[256,768]{1,0:T(8,128)(2,1)S(1)} %get-tuple-element.16), channel_id=1, source_target_pairs={{2,0},{4,2},{6,4},{8,6},{10,8},{12,10},{14,12},{3,1},{5,3},{7,5},{... | collective-permute-start | bytes 1179656 | tf_op jit(solution)/shard_map/ppermute | solution.py:571
  85.9 45.3 %collective-permute-start.5 = (bf16[384,768]{1,0:T(8,128)(2,1)S(1)}, bf16[384,768]{1,0:T(8,128)(2,1)S(1)}, u32[]{:S(2)}, u32[]{:S(2)}) collective-permute-start(bf16[384,768]{1,0:T(8,128)(2,1)S(1)} %collective-permute-done.4.own_cross), channel_id=1, source_target_pairs={{0,1},{1,0},{2,3},{3,2},{4,5},{5,4},{6,7},{7,6},{8,9},{9,8},{10,11... | collective-permute-start | bytes 1769480 | tf_op jit(solution)/shard_map/ppermute | solution.py:566
  94.7 25.2 %collective-permute-start.7 = (bf16[256,768]{1,0:T(8,128)(2,1)S(1)}, bf16[256,768]{1,0:T(8,128)(2,1)S(1)}, u32[]{:S(2)}, u32[]{:S(2)}) collective-permute-start(bf16[256,768]{1,0:T(8,128)(2,1)S(1)} %get-tuple-element.14), channel_id=1, source_target_pairs={{2,0},{4,2},{6,4},{8,6},{10,8},{12,10},{14,12},{3,1},{5,3},{7,5},{... | collective-permute-start | bytes 1179656 | tf_op jit(solution)/shard_map/ppermute | solution.py:571
  103.0 18.2 %collective-permute-start.15 = (bf16[400,384]{1,0:T(8,128)(2,1)S(1)}, bf16[400,384]{1,0:T(8,128)(2,1)S(1)}, u32[]{:S(2)}, u32[]{:S(2)}) collective-permute-start(bf16[400,384]{1,0:T(8,128)(2,1)S(1)} %broadcast_select_fusion.own_sum), channel_id=1, source_target_pairs={{0,1},{1,0},{2,3},{3,2},{4,5},{5,4},{6,7},{7,6},{8,9},{9,8},{10,11... | collective-permute-start | bytes 921608 | tf_op jit(solution)/shard_map/ppermute | solution.py:566
  103.0 28.2 %collective-permute-start.2 = (bf16[400,384]{1,0:T(8,128)(2,1)}, bf16[400,384]{1,0:T(8,128)(2,1)S(1)}, u32[]{:S(2)}, u32[]{:S(2)}) collective-permute-start(bf16[400,384]{1,0:T(8,128)(2,1)} %copy-done.3), channel_id=1, source_target_pairs={{2,0},{4,2},{6,4},{8,6},{10,8},{12,10},{14,12},{3,1},{5,3},{7,5},{... | collective-permute-start | bytes 921608 | tf_op jit(solution)/shard_map/ppermute | solution.py:571
  111.4 9.8 %copy-start.1 = (bf16[768,384]{1,0:T(8,128)(2,1)S(1)}, bf16[768,384]{1,0:T(8,128)(2,1)}, u32[]{:S(2)}) copy-start(bf16[768,384]{1,0:T(8,128)(2,1)} %tip.1) | copy-start | bytes 1769476
  111.5 19.8 %collective-permute-start.1 = (bf16[384,384]{1,0:T(8,128)(2,1)}, bf16[384,384]{1,0:T(8,128)(2,1)S(1)}, u32[]{:S(2)}, u32[]{:S(2)}) collective-permute-start(bf16[384,384]{1,0:T(8,128)(2,1)} %copy-done.4), channel_id=1, source_target_pairs={{2,0},{4,2},{6,4},{8,6},{10,8},{12,10},{14,12},{3,1},{5,3},{7,5},{... | collective-permute-start | bytes 884744 | tf_op jit(solution)/shard_map/ppermute | solution.py:571
  114.3 16.9 %copy-start = (bf16[1536,768]{1,0:T(8,128)(2,1)S(1)}, bf16[1536,768]{1,0:T(8,128)(2,1)}, u32[]{:S(2)}) copy-start(bf16[1536,768]{1,0:T(8,128)(2,1)} %separator.1) | copy-start | bytes 7077892

commit v2 on v1

--- a/solution.py
+++ b/solution.py
@@ -15,7 +15,7 @@
 MOST_STEPS = 60
 STAGES = 7
 PAD = 16
-PIECES = 3
+PIECES = (3, 2, 1)
 
 
 def split(x):
@@ -376,9 +376,13 @@
     )(flags, own_r, other_r)
 
 
+def starts(rows):
+    return [sum(PIECES[:i]) * rows // sum(PIECES) for i in range(len(PIECES) + 1)]
+
+
 def arrow_kernel(flags, own_r, other_r, own_e, *outs):
     rows = own_r.shape[0]
-    share = 2 * rows // len(outs)
+    bounds = starts(2 * rows)
     active, core = flags[2], flags[1]
 
     @pl.when(active == 0)
@@ -390,9 +394,10 @@
         for source, base in ((first, 0), (second, rows)):
             value = (-nn(source[...], own_e[...])).astype(BF16)
             for i, out in enumerate(outs):
-                low, high = max(base, i * share), min(base + rows, (i + 1) * share)
+                begin = bounds[i]
+                low, high = max(base, begin), min(base + rows, bounds[i + 1])
                 if low < high:
-                    out[low - i * share:high - i * share, :] = value[low - base:high - base, :]
+                    out[low - begin:high - begin, :] = value[low - base:high - base, :]
 
     @pl.when(jnp.logical_and(active != 0, core == 0))
     def _():
@@ -404,12 +409,15 @@
 
 
 def arrow_terms(flags, own_r, other_r, own_e):
-    piece = jax.ShapeDtypeStruct((2 * own_r.shape[0] // PIECES, own_e.shape[1]), BF16)
+    bounds = starts(2 * own_r.shape[0])
     return pl.pallas_call(
         arrow_kernel,
-        out_shape=(piece,) * PIECES,
+        out_shape=tuple(
+            jax.ShapeDtypeStruct((high - low, own_e.shape[1]), BF16)
+            for low, high in zip(bounds, bounds[1:])
+        ),
         in_specs=[SMEM, VMEM, VMEM, VMEM],
-        out_specs=(VMEM,) * PIECES,
+        out_specs=(VMEM,) * len(PIECES),
         compiler_params=params(24),
         cost_estimate=cost(2 * 10**9, 6 * 2**20),
     )(flags, own_r, other_r, own_e)
@@ -520,14 +528,14 @@
 
 def rows_kernel(count, flags, *refs):
     sources, out, sem = refs[:count], refs[-2], refs[-1]
-    share = sources[0].shape[0]
+    bounds = starts(out.shape[0])
 
     def copy(source, i):
-        place = out.at[i * share:(i + 1) * share, :]
+        place = out.at[bounds[i]:bounds[i + 1], :]
         return pltpu.make_async_copy(source, place, sem.at[i])
 
     if count == 1:
-        last = out.shape[0] // share - 1
+        last = len(PIECES) - 1
         copy(sources[0], last).start()
         copy(sources[0], last).wait()
         return
@@ -555,7 +563,7 @@
         out_shape=jax.ShapeDtypeStruct(shape, BF16),
         in_specs=[SMEM] + [VMEM] * count + [ANY] * len(more),
         out_specs=ANY,
-        scratch_shapes=[pltpu.SemaphoreType.DMA((PIECES,))],
+        scratch_shapes=[pltpu.SemaphoreType.DMA((len(PIECES),))],
         input_output_aliases={count + 1: 0} if more else {},
         compiler_params=params(16),
         cost_estimate=cost(10**6, 2 * 2**20),

time: 134 us -> 138 us (1.030)
  the two profiles are of different devices: /device:TPU:0 before, /device:TPU:2 now
where the time goes in v2:
time: 138 us; the launch traced here: 137 us
  waiting for transfers between devices  88.4 us (64%)
  starting transfers between devices  30.2 us (22%)
  Pallas kernels  12.4 us (9%)
  other arithmetic  2.04 us (1%)
  local copies, waits for them, and re-layouts  1.98 us (1%)
  between operations  1.57 us (1%)
    ppermute x1, waiting for transfers between devices, summed(): lax.ppermute(term, 'tm', [(i, i + 1) for i in range(0, count, 2)])  33.1 us
    ppermute x5, waiting for transfers between devices, to_previous(): return lax.ppermute(x, 'tm', [(i, i - 1) for i in range(1, count)])  18.5 us
    ppermute x1, waiting for transfers between devices, summed(): lax.ppermute(term, 'tm', [(i + 1, i) for i in range(0, count, 2)])  16.1 us
    ppermute x2, waiting for transfers between devices, summed(): term = added(term, lax.ppermute(term, 'tm', pairs))  15.4 us
    ppermute x5, starting transfers between devices, to_previous(): return lax.ppermute(x, 'tm', [(i, i - 1) for i in range(1, count)])  12.1 us
    ppermute x2, starting transfers between devices, summed(): term = added(term, lax.ppermute(term, 'tm', pairs))  11.5 us
    ppermute x5, waiting for transfers between devices, swapped(): return lax.ppermute(x, 'space', [(0, 1), (1, 0)])  5.21 us
  transfers between devices with their start and end apart: 16, of which 8 were waited for; matrix products, arithmetic and copies ran while one was open for 2% of the time, Pallas kernels for 5%

profile of v2, /device:TPU:2, one launch (start us, length us, event | category | flops | bytes accessed | tf_op | source)
XLA Modules:
  0.0 136.5 jit_solution(3240191125256549765)
XLA Ops:
  0.7 1.2 dynamic_slice.3
  2.7 2.9 %collective-permute-done.other_d = bf16[1536,768]{1,0:T(8,128)(2,1)} collective-permute-done((bf16[1536,768]{1,0:T(8,128)(2,1)}, bf16[1536,768]{1,0:T(8,128)(2,1)}, u32[]{:S(2)}, u32[]{:S(2)}) %collective-permute-start) | collective-permute-done | bytes 2359328 | tf_op jit(solution)/shard_map/ppermute | solution.py:574
  5.6 2.6 %shard_map.85 = (bf16[1536,768]{1,0:T(8,128)(2,1)}, bf16[384,1536]{1,0:T(8,128)(2,1)S(1)}, bf16[384,384]{1,0:T(8,128)(2,1)S(1)}, bf16[400,384]{1,0:T(8,128)(2,1)S(1)}) custom-call(s32[4]{0:T(128)S(1)} %add_convert_fusion.3.flags, bf16[1536,768]{1,0:T(8,128)(2,1)} %own_d.1, bf16[1536,768]{1,0:T(8,128)(2,1)} %collective-permute-done.other_d, ...), custom_call_target="tpu_custom_call" | custom-call | flops 28000000000 | bytes 16777216 | tf_op jit(solution)/shard_map/pallas_call | solution.py:314
  8.2 0.7 copy-done.3
  9.1 0.4 collective-permute-start.3
  9.5 2.3 %collective-permute-done.6.other_r = bf16[384,1536]{1,0:T(8,128)(2,1)S(1)} collective-permute-done((bf16[384,1536]{1,0:T(8,128)(2,1)S(1)}, bf16[384,1536]{1,0:T(8,128)(2,1)S(1)}, u32[]{:S(2)}, u32[]{:S(2)}) %collective-permute-start.6) | collective-permute-done | bytes 1179680 | tf_op jit(solution)/shard_map/ppermute | solution.py:574
  11.8 0.6 shard_map.91
  12.4 1.3 collective-permute-start.11
  13.7 33.1 %collective-permute-done.11 = bf16[400,384]{1,0:T(8,128)(2,1)S(1)} collective-permute-done((bf16[400,384]{1,0:T(8,128)(2,1)S(1)}, bf16[400,384]{1,0:T(8,128)(2,1)S(1)}, u32[]{:S(2)}, u32[]{:S(2)}) %collective-permute-start.11) | collective-permute-done | bytes 307232 | tf_op jit(solution)/shard_map/ppermute | solution.py:593
  46.9 7.0 %collective-permute-start.12 = (bf16[400,384]{1,0:T(8,128)(2,1)S(1)}, bf16[400,384]{1,0:T(8,128)(2,1)S(1)}, u32[]{:S(2)}, u32[]{:S(2)}) collective-permute-start(bf16[400,384]{1,0:T(8,128)(2,1)S(1)} %add_convert_fusion.2), channel_id=1, source_target_pairs={{2,6},{6,2},{10,14},{14,10},{3,7},{7,3},{11,15},{15,11},{18,22},{2... | collective-permute-start | bytes 921608 | tf_op jit(solution)/shard_map/ppermute | solution.py:597
  53.9 7.3 %collective-permute-done.12 = bf16[400,384]{1,0:T(8,128)(2,1)S(1)} collective-permute-done((bf16[400,384]{1,0:T(8,128)(2,1)S(1)}, bf16[400,384]{1,0:T(8,128)(2,1)S(1)}, u32[]{:S(2)}, u32[]{:S(2)}) %collective-permute-start.12) | collective-permute-done | bytes 307232 | tf_op jit(solution)/shard_map/ppermute | solution.py:597
  61.3 4.5 %collective-permute-start.13 = (bf16[400,384]{1,0:T(8,128)(2,1)S(1)}, bf16[400,384]{1,0:T(8,128)(2,1)S(1)}, u32[]{:S(2)}, u32[]{:S(2)}) collective-permute-start(bf16[400,384]{1,0:T(8,128)(2,1)S(1)} %add_convert_fusion.1), channel_id=1, source_target_pairs={{2,10},{6,14},{10,2},{14,6},{3,11},{7,15},{11,3},{15,7},{18,26},{2... | collective-permute-start | bytes 921608 | tf_op jit(solution)/shard_map/ppermute | solution.py:597
  65.9 0.6 shard_map.86
  66.5 1.9 %collective-permute-start.4 = (bf16[384,768]{1,0:T(8,128)(2,1)S(1)}, bf16[384,768]{1,0:T(8,128)(2,1)S(1)}, u32[]{:S(2)}, u32[]{:S(2)}) collective-permute-start(bf16[384,768]{1,0:T(8,128)(2,1)S(1)} %shard_map.86), channel_id=1, source_target_pairs={{2,0},{4,2},{6,4},{8,6},{10,8},{12,10},{14,12},{3,1},{5,3},{7,5},{... | collective-permute-start | bytes 1769480 | tf_op jit(solution)/shard_map/ppermute | solution.py:579
  68.4 1.4 %shard_map.88 = (bf16[384,768]{1,0:T(8,128)(2,1)S(1)}, bf16[256,768]{1,0:T(8,128)(2,1)}, bf16[128,768]{1,0:T(8,128)(2,1)S(1)}) custom-call(s32[4]{0:T(128)S(1)} %add_convert_fusion.3.flags, bf16[384,1536]{1,0:T(8,128)(2,1)S(1)} %get-tuple-element.13.own_r, bf16[384,1536]{1,0:T(8,128)(2,1)S(1)} %collective-permute-done.6.other_r, bf16[1536,768]{1,0:T(8,128)(2,1)S(1)} %copy-done.2), custom_call_target="tpu_custom_call" | custom-call | flops 2000000000 | bytes 6291456 | tf_op jit(solution)/shard_map/pallas_call | solution.py:413
  69.8 1.3 collective-permute-start.8
  71.1 8.1 %collective-permute-done.13 = bf16[400,384]{1,0:T(8,128)(2,1)S(1)} collective-permute-done((bf16[400,384]{1,0:T(8,128)(2,1)S(1)}, bf16[400,384]{1,0:T(8,128)(2,1)S(1)}, u32[]{:S(2)}, u32[]{:S(2)}) %collective-permute-start.13) | collective-permute-done | bytes 307232 | tf_op jit(solution)/shard_map/ppermute | solution.py:597
  79.2 0.8 add_convert_fusion
  80.0 2.0 %collective-permute-start.14 = (bf16[400,384]{1,0:T(8,128)(2,1)}, bf16[400,384]{1,0:T(8,128)(2,1)}, u32[]{:S(2)}, u32[]{:S(2)}) collective-permute-start(bf16[400,384]{1,0:T(8,128)(2,1)} %add_convert_fusion), channel_id=1, source_target_pairs={{2,0},{6,4},{10,8},{14,12},{3,1},{7,5},{11,9},{15,13},{18,16},{22,... | collective-permute-start | bytes 921608 | tf_op jit(solution)/shard_map/ppermute | solution.py:599
  82.0 1.3 collective-permute-start.9
  83.3 1.9 %collective-permute-start.10 = (bf16[256,768]{1,0:T(8,128)(2,1)}, bf16[256,768]{1,0:T(8,128)(2,1)S(1)}, u32[]{:S(2)}, u32[]{:S(2)}) collective-permute-start(bf16[256,768]{1,0:T(8,128)(2,1)} %get-tuple-element.16), channel_id=1, source_target_pairs={{2,0},{4,2},{6,4},{8,6},{10,8},{12,10},{14,12},{3,1},{5,3},{7,5},{... | collective-permute-start | bytes 1179656 | tf_op jit(solution)/shard_map/ppermute | solution.py:579
  85.3 16.1 %collective-permute-done.14 = bf16[400,384]{1,0:T(8,128)(2,1)} collective-permute-done((bf16[400,384]{1,0:T(8,128)(2,1)}, bf16[400,384]{1,0:T(8,128)(2,1)}, u32[]{:S(2)}, u32[]{:S(2)}) %collective-permute-start.14) | collective-permute-done | bytes 307232 | tf_op jit(solution)/shard_map/ppermute | solution.py:599
  101.4 1.0 broadcast_select_fusion.own_sum
  102.5 5.7 %collective-permute-done.10.refs_2_ = bf16[256,768]{1,0:T(8,128)(2,1)S(1)} collective-permute-done((bf16[256,768]{1,0:T(8,128)(2,1)}, bf16[256,768]{1,0:T(8,128)(2,1)S(1)}, u32[]{:S(2)}, u32[]{:S(2)}) %collective-permute-start.10) | collective-permute-done | bytes 393248 | tf_op jit(solution)/shard_map/ppermute | solution.py:579
  108.2 4.3 %collective-permute-start.2 = (bf16[400,384]{1,0:T(8,128)(2,1)}, bf16[400,384]{1,0:T(8,128)(2,1)S(1)}, u32[]{:S(2)}, u32[]{:S(2)}) collective-permute-start(bf16[400,384]{1,0:T(8,128)(2,1)} %copy-done.3), channel_id=1, source_target_pairs={{2,0},{4,2},{6,4},{8,6},{10,8},{12,10},{14,12},{3,1},{5,3},{7,5},{... | collective-permute-start | bytes 921608 | tf_op jit(solution)/shard_map/ppermute | solution.py:579
  112.5 1.9 %collective-permute-start.1 = (bf16[384,384]{1,0:T(8,128)(2,1)}, bf16[384,384]{1,0:T(8,128)(2,1)S(1)}, u32[]{:S(2)}, u32[]{:S(2)}) collective-permute-start(bf16[384,384]{1,0:T(8,128)(2,1)} %copy-done.4), channel_id=1, source_target_pairs={{2,0},{4,2},{6,4},{8,6},{10,8},{12,10},{14,12},{3,1},{5,3},{7,5},{... | collective-permute-start | bytes 884744 | tf_op jit(solution)/shard_map/ppermute | solution.py:579
  114.5 2.1 %collective-permute-start.7 = (bf16[128,768]{1,0:T(8,128)(2,1)S(1)}, bf16[128,768]{1,0:T(8,128)(2,1)S(1)}, u32[]{:S(2)}, u32[]{:S(2)}) collective-permute-start(bf16[128,768]{1,0:T(8,128)(2,1)S(1)} %get-tuple-element.14), channel_id=1, source_target_pairs={{2,0},{4,2},{6,4},{8,6},{10,8},{12,10},{14,12},{3,1},{5,3},{7,5},{... | collective-permute-start | bytes 589832 | tf_op jit(solution)/shard_map/ppermute | solution.py:579
  116.5 1.5 %shard_map.89.refs_1_ = bf16[768,768]{1,0:T(8,128)(2,1)} custom-call(s32[4]{0:T(128)S(1)} %add_convert_fusion.3.flags, bf16[384,768]{1,0:T(8,128)(2,1)S(1)} %collective-permute-done.8.refs_0_, bf16[384,768]{1,0:T(8,128)(2,1)S(1)} %collective-permute-done.9.refs_1_, bf16[256,768]{1,0:T(8,128)(2,1)S(1)} %collective-permute-done.10.refs_2_), custom_call_target="tpu_custom_call" | custom-call | flops 1000000 | bytes 2097152 | tf_op jit(solution)/shard_map/pallas_call | solution.py:561
  118.1 12.8 %collective-permute-done.7.refs_0_ = bf16[128,768]{1,0:T(8,128)(2,1)S(1)} collective-permute-done((bf16[128,768]{1,0:T(8,128)(2,1)S(1)}, bf16[128,768]{1,0:T(8,128)(2,1)S(1)}, u32[]{:S(2)}, u32[]{:S(2)}) %collective-permute-start.7) | collective-permute-done | bytes 196640 | tf_op jit(solution)/shard_map/ppermute | solution.py:579
  130.8 1.2 shard_map.90
  132.1 1.8 %shard_map.92 = f32[768,384]{1,0:T(8,128)} custom-call(s32[4]{0:T(128)S(1)} %add_convert_fusion.3.flags, bf16[768,384]{1,0:T(8,128)(2,1)S(1)} %copy-done.1, bf16[400,384]{1,0:T(8,128)(2,1)S(1)} %broadcast_select_fusion.own_sum, bf16[400,384]{1,0:T(8,128)(2,1)S(1)} %collective-permute-done.15.other_sum), custom_call_target="tpu_custom_call" | custom-call | flops 1000000 | bytes 3145728 | tf_op jit(solution)/shard_map/pallas_call | solution.py:519
  133.9 2.6 %shard_map.87 = bf16[1536,768]{1,0:T(8,128)(2,1)} custom-call(s32[4]{0:T(128)S(1)} %add_convert_fusion.3.flags, bf16[1536,768]{1,0:T(8,128)(2,1)S(1)} %copy-done, bf16[384,384]{1,0:T(8,128)(2,1)S(1)} %collective-permute-done.1.corner_in, bf16[400,384]{1,0:T(8,128)(2,1)S(1)} %collective-permute-done.2.folded, ...), custom_call_target="tpu_custom_call" | custom-call | flops 1000000 | bytes 6291456 | tf_op jit(solution)/shard_map/pallas_call | solution.py:487
  (24 shorter events, 0.6 us)
Async XLA Ops:
  0.6 4.9 %collective-permute-start = (bf16[1536,768]{1,0:T(8,128)(2,1)}, bf16[1536,768]{1,0:T(8,128)(2,1)}, u32[]{:S(2)}, u32[]{:S(2)}) collective-permute-start(bf16[1536,768]{1,0:T(8,128)(2,1)} %own_d.1), channel_id=1, source_target_pairs={{0,1},{1,0},{2,3},{3,2},{4,5},{5,4},{6,7},{7,6},{8,9},{9,8},{10,11... | collective-permute-start | bytes 7077896 | tf_op jit(solution)/shard_map/ppermute | solution.py:574
  8.2 0.7 copy-start.3
  8.9 52.4 %copy-start.4 = (bf16[384,384]{1,0:T(8,128)(2,1)}, bf16[384,384]{1,0:T(8,128)(2,1)S(1)}, u32[]{:S(2)}) copy-start(bf16[384,384]{1,0:T(8,128)(2,1)S(1)} %get-tuple-element.10) | copy-start | bytes 884740
  8.9 2.8 %collective-permute-start.6 = (bf16[384,1536]{1,0:T(8,128)(2,1)S(1)}, bf16[384,1536]{1,0:T(8,128)(2,1)S(1)}, u32[]{:S(2)}, u32[]{:S(2)}) collective-permute-start(bf16[384,1536]{1,0:T(8,128)(2,1)S(1)} %get-tuple-element.13.own_r), channel_id=1, source_target_pairs={{0,1},{1,0},{2,3},{3,2},{4,5},{5,4},{6,7},{7,6},{8,9},{9,8},{10,11... | collective-permute-start | bytes 3538952 | tf_op jit(solution)/shard_map/ppermute | solution.py:574
  9.1 56.8 %copy-start.2 = (bf16[1536,768]{1,0:T(8,128)(2,1)S(1)}, bf16[1536,768]{1,0:T(8,128)(2,1)}, u32[]{:S(2)}) copy-start(bf16[1536,768]{1,0:T(8,128)(2,1)} %get-tuple-element.12.own_e) | copy-start | bytes 7077892
  9.1 56.8 %collective-permute-start.3 = (bf16[1536,768]{1,0:T(8,128)(2,1)}, bf16[1536,768]{1,0:T(8,128)(2,1)S(1)}, u32[]{:S(2)}, u32[]{:S(2)}) collective-permute-start(bf16[1536,768]{1,0:T(8,128)(2,1)} %get-tuple-element.12.own_e), channel_id=1, source_target_pairs={{0,1},{1,0},{2,3},{3,2},{4,5},{5,4},{6,7},{7,6},{8,9},{9,8},{10,11... | collective-permute-start | bytes 7077896 | tf_op jit(solution)/shard_map/ppermute | solution.py:574
  12.4 34.4 %collective-permute-start.11 = (bf16[400,384]{1,0:T(8,128)(2,1)S(1)}, bf16[400,384]{1,0:T(8,128)(2,1)S(1)}, u32[]{:S(2)}, u32[]{:S(2)}) collective-permute-start(bf16[400,384]{1,0:T(8,128)(2,1)S(1)} %shard_map.91), channel_id=1, source_target_pairs={{0,2},{4,6},{8,10},{12,14},{1,3},{5,7},{9,11},{13,15},{16,18},{20,... | collective-permute-start | bytes 921608 | tf_op jit(solution)/shard_map/ppermute | solution.py:593
  46.9 14.3 %collective-permute-start.12 = (bf16[400,384]{1,0:T(8,128)(2,1)S(1)}, bf16[400,384]{1,0:T(8,128)(2,1)S(1)}, u32[]{:S(2)}, u32[]{:S(2)}) collective-permute-start(bf16[400,384]{1,0:T(8,128)(2,1)S(1)} %add_convert_fusion.2), channel_id=1, source_target_pairs={{2,6},{6,2},{10,14},{14,10},{3,7},{7,3},{11,15},{15,11},{18,22},{2... | collective-permute-start | bytes 921608 | tf_op jit(solution)/shard_map/ppermute | solution.py:597
  61.3 17.9 %collective-permute-start.13 = (bf16[400,384]{1,0:T(8,128)(2,1)S(1)}, bf16[400,384]{1,0:T(8,128)(2,1)S(1)}, u32[]{:S(2)}, u32[]{:S(2)}) collective-permute-start(bf16[400,384]{1,0:T(8,128)(2,1)S(1)} %add_convert_fusion.1), channel_id=1, source_target_pairs={{2,10},{6,14},{10,2},{14,6},{3,11},{7,15},{11,3},{15,7},{18,26},{2... | collective-permute-start | bytes 921608 | tf_op jit(solution)/shard_map/ppermute | solution.py:597
  66.5 18.7 %collective-permute-start.4 = (bf16[384,768]{1,0:T(8,128)(2,1)S(1)}, bf16[384,768]{1,0:T(8,128)(2,1)S(1)}, u32[]{:S(2)}, u32[]{:S(2)}) collective-permute-start(bf16[384,768]{1,0:T(8,128)(2,1)S(1)} %shard_map.86), channel_id=1, source_target_pairs={{2,0},{4,2},{6,4},{8,6},{10,8},{12,10},{14,12},{3,1},{5,3},{7,5},{... | collective-permute-start | bytes 1769480 | tf_op jit(solution)/shard_map/ppermute | solution.py:579
  69.8 42.7 %collective-permute-start.8 = (bf16[384,768]{1,0:T(8,128)(2,1)S(1)}, bf16[384,768]{1,0:T(8,128)(2,1)S(1)}, u32[]{:S(2)}, u32[]{:S(2)}) collective-permute-start(bf16[384,768]{1,0:T(8,128)(2,1)S(1)} %get-tuple-element.15), channel_id=1, source_target_pairs={{2,0},{6,4},{10,8},{14,12},{3,1},{7,5},{11,9},{15,13},{18,16},{22,... | collective-permute-start | bytes 1769480 | tf_op jit(solution)/shard_map/ppermute | solution.py:584
  80.0 21.4 %collective-permute-start.14 = (bf16[400,384]{1,0:T(8,128)(2,1)}, bf16[400,384]{1,0:T(8,128)(2,1)}, u32[]{:S(2)}, u32[]{:S(2)}) collective-permute-start(bf16[400,384]{1,0:T(8,128)(2,1)} %add_convert_fusion), channel_id=1, source_target_pairs={{2,0},{6,4},{10,8},{14,12},{3,1},{7,5},{11,9},{15,13},{18,16},{22,... | collective-permute-start | bytes 921608 | tf_op jit(solution)/shard_map/ppermute | solution.py:599
  82.0 32.4 %collective-permute-start.9 = (bf16[384,768]{1,0:T(8,128)(2,1)S(1)}, bf16[384,768]{1,0:T(8,128)(2,1)S(1)}, u32[]{:S(2)}, u32[]{:S(2)}) collective-permute-start(bf16[384,768]{1,0:T(8,128)(2,1)S(1)} %get-tuple-element.15), channel_id=1, source_target_pairs={{4,2},{8,6},{12,10},{5,3},{9,7},{13,11},{20,18},{24,22},{28,26},{2... | collective-permute-start | bytes 1769480 | tf_op jit(solution)/shard_map/ppermute | solution.py:584
  83.3 24.9 %collective-permute-start.10 = (bf16[256,768]{1,0:T(8,128)(2,1)}, bf16[256,768]{1,0:T(8,128)(2,1)S(1)}, u32[]{:S(2)}, u32[]{:S(2)}) collective-permute-start(bf16[256,768]{1,0:T(8,128)(2,1)} %get-tuple-element.16), channel_id=1, source_target_pairs={{2,0},{4,2},{6,4},{8,6},{10,8},{12,10},{14,12},{3,1},{5,3},{7,5},{... | collective-permute-start | bytes 1179656 | tf_op jit(solution)/shard_map/ppermute | solution.py:579
  85.2 48.7 %collective-permute-start.5 = (bf16[384,768]{1,0:T(8,128)(2,1)S(1)}, bf16[384,768]{1,0:T(8,128)(2,1)S(1)}, u32[]{:S(2)}, u32[]{:S(2)}) collective-permute-start(bf16[384,768]{1,0:T(8,128)(2,1)S(1)} %collective-permute-done.4.own_cross), channel_id=1, source_target_pairs={{0,1},{1,0},{2,3},{3,2},{4,5},{5,4},{6,7},{7,6},{8,9},{9,8},{10,11... | collective-permute-start | bytes 1769480 | tf_op jit(solution)/shard_map/ppermute | solution.py:574
  102.4 29.6 %collective-permute-start.15 = (bf16[400,384]{1,0:T(8,128)(2,1)S(1)}, bf16[400,384]{1,0:T(8,128)(2,1)S(1)}, u32[]{:S(2)}, u32[]{:S(2)}) collective-permute-start(bf16[400,384]{1,0:T(8,128)(2,1)S(1)} %broadcast_select_fusion.own_sum), channel_id=1, source_target_pairs={{0,1},{1,0},{2,3},{3,2},{4,5},{5,4},{6,7},{7,6},{8,9},{9,8},{10,11... | collective-permute-start | bytes 921608 | tf_op jit(solution)/shard_map/ppermute | solution.py:574
  108.2 25.7 %collective-permute-start.2 = (bf16[400,384]{1,0:T(8,128)(2,1)}, bf16[400,384]{1,0:T(8,128)(2,1)S(1)}, u32[]{:S(2)}, u32[]{:S(2)}) collective-permute-start(bf16[400,384]{1,0:T(8,128)(2,1)} %copy-done.3), channel_id=1, source_target_pairs={{2,0},{4,2},{6,4},{8,6},{10,8},{12,10},{14,12},{3,1},{5,3},{7,5},{... | collective-permute-start | bytes 921608 | tf_op jit(solution)/shard_map/ppermute | solution.py:579
  112.5 21.4 %collective-permute-start.1 = (bf16[384,384]{1,0:T(8,128)(2,1)}, bf16[384,384]{1,0:T(8,128)(2,1)S(1)}, u32[]{:S(2)}, u32[]{:S(2)}) collective-permute-start(bf16[384,384]{1,0:T(8,128)(2,1)} %copy-done.4), channel_id=1, source_target_pairs={{2,0},{4,2},{6,4},{8,6},{10,8},{12,10},{14,12},{3,1},{5,3},{7,5},{... | collective-permute-start | bytes 884744 | tf_op jit(solution)/shard_map/ppermute | solution.py:579
  114.5 17.6 %copy-start.1 = (bf16[768,384]{1,0:T(8,128)(2,1)S(1)}, bf16[768,384]{1,0:T(8,128)(2,1)}, u32[]{:S(2)}) copy-start(bf16[768,384]{1,0:T(8,128)(2,1)} %tip.1) | copy-start | bytes 1769476
  114.5 16.4 %collective-permute-start.7 = (bf16[128,768]{1,0:T(8,128)(2,1)S(1)}, bf16[128,768]{1,0:T(8,128)(2,1)S(1)}, u32[]{:S(2)}, u32[]{:S(2)}) collective-permute-start(bf16[128,768]{1,0:T(8,128)(2,1)S(1)} %get-tuple-element.14), channel_id=1, source_target_pairs={{2,0},{4,2},{6,4},{8,6},{10,8},{12,10},{14,12},{3,1},{5,3},{7,5},{... | collective-permute-start | bytes 589832 | tf_op jit(solution)/shard_map/ppermute | solution.py:579
  118.0 15.9 %copy-start = (bf16[1536,768]{1,0:T(8,128)(2,1)S(1)}, bf16[1536,768]{1,0:T(8,128)(2,1)}, u32[]{:S(2)}) copy-start(bf16[1536,768]{1,0:T(8,128)(2,1)} %separator.1) | copy-start | bytes 7077892
